TPU v7x, 128 devices: a whole 4x4x4 slice. The times are simulated.
128 devices in a mesh: range: 16 (over z, y), doppler: 8 (over x, core).
Axes of the slice: x: 4, y: 4, z: 4, core: 2. Of those that a mesh axis runs over, the one named last changes fastest.
Arguments:
- snapshots: bfloat16 [128, 16384, 384], P(None, ('range', 'doppler')), may hold values from -24 to 24
- steering: bfloat16 [128, 384, 256], P(('range', 'doppler')), may hold values from -0.3125 to 0.3125
- train_list: int32 [128, 128], P(('range', 'doppler')), may hold values from 0 to 127, each once within a row
- train_count: int32 [128], P(('range', 'doppler')), may hold values from 42 to 128, as said below
Outputs:
- beam_output: bfloat16 [128, 16384, 256], P(None, ('range', 'doppler'))
Inputs may be any that keep to these rules, and one draw needn't show every extreme that they name: `train_count`: some bin trains on all 128 blocks and some bin on 42.
All inputs are finite; a program needn't handle non-finite values.
Results may differ from a plain program's by a relative error of at most 0.0052.
Values may be sent and summed in bfloat16 or wider, within the bound.
A program may use at most 128 MiB of HBM per device.

v0:
```python
import jax
import jax.numpy as jnp
from jax import lax
from jax.sharding import PartitionSpec as P

BLOCK = 128


LOADING = 0.1


def selection(train_list, train_count):
    block_total = train_list.shape[1]
    position = lax.broadcasted_iota(jnp.int32, (1, block_total, 1), 1)
    block_ids = lax.broadcasted_iota(jnp.int32, (1, 1, block_total), 2)
    matches = (train_list[:, :, None] == block_ids) & (position < train_count[:, None, None])
    return jnp.sum(matches.astype(jnp.int32), axis=1)


def solve_one(factor, rhs_block):
    inner = lax.linalg.triangular_solve(factor, rhs_block, left_side=True, lower=True)
    return lax.linalg.triangular_solve(factor, inner, left_side=True, lower=True, transpose_a=True)


def adapt(own_snaps, train_list, train_count, steering):
    own_bins, gate_total, channels = own_snaps.shape
    block_total = train_list.shape[1]
    chosen = selection(train_list, train_count)
    blocks = own_snaps.reshape(own_bins, block_total, gate_total // block_total, channels)
    masked = blocks * chosen.astype(own_snaps.dtype)[:, :, None, None]
    gram_sum = jnp.einsum("bnrd,bnre->bde", masked, blocks, preferred_element_type=jnp.float32)
    scale = (BLOCK * train_count).astype(jnp.float32)
    covariance = (
        gram_sum / scale[:, None, None] + LOADING * jnp.eye(channels, dtype=jnp.float32)[None]
    )
    factor = jnp.linalg.cholesky(covariance)
    steer_full = steering.astype(jnp.float32)
    solved = jax.vmap(solve_one)(factor, steer_full)
    response = jnp.sum(steer_full * solved, axis=1)
    return (solved / response[:, None, :]).astype(jnp.bfloat16)


def body(snapshots, steering, train_list, train_count):
    bin_total, gate_rows, channels = snapshots.shape
    own_bins = steering.shape[0]
    devices = bin_total // own_bins
    outgoing = snapshots.reshape(devices, own_bins, gate_rows, channels)
    arrived = lax.all_to_all(
        outgoing, ("range", "doppler"), split_axis=0, concat_axis=0, tiled=True
    )
    own_snaps = jnp.moveaxis(arrived, 1, 0).reshape(own_bins, devices * gate_rows, channels)
    weights = adapt(own_snaps, train_list, train_count, steering)
    return jnp.einsum(
        "bgd,bde->bge",
        snapshots,
        lax.all_gather(weights, ("range", "doppler"), axis=0, tiled=True),
        preferred_element_type=jnp.float32,
    ).astype(jnp.bfloat16)


def solution(mesh):
    placed = (
        P(None, ("range", "doppler"), None),
        P(("range", "doppler"), None, None),
        P(("range", "doppler"), None),
        P(("range", "doppler")),
    )
    return jax.shard_map(
        body,
        mesh=mesh,
        in_specs=placed,
        out_specs=P(None, ("range", "doppler"), None),
        check_vma=False,
    )
```

profile of v0, /device:TPU:1, one launch (start us, length us, event | category | flops | bytes accessed | tf_op | source)
XLA Modules:
  0.0 431.1 jit_solution(15140216038816594535)
XLA Ops:
  6.5 11.9 %all-to-all-start = ((bf16[128,1,128,384]{3,2,1,0:T(8,128)(2,1)}), bf16[128,1,128,384]{3,2,1,0:T(8,128)(2,1)}, u32[]{:S(2)}, u32[]{:S(2)}) async-start(bf16[128,1,128,384]{3,2,1,0:T(8,128)(2,1)} %bitcast.154), calls=%async_computation | async-start | bytes 25165824 | tf_op jit(solution)/shard_map/all_to_all | solution.py:48
  19.4 150.7 %all-to-all-done = bf16[128,1,128,384]{3,2,1,0:T(8,128)(2,1)} async-done(((bf16[128,1,128,384]{3,2,1,0:T(8,128)(2,1)}), bf16[128,1,128,384]{3,2,1,0:T(8,128)(2,1)}, u32[]{:S(2)}, u32[]{:S(2)}) %all-to-all-start) | async-done | bytes 12582944 | tf_op jit(solution)/shard_map/all_to_all | solution.py:48
  170.0 14.2 %fusion.22 = f32[384,384]{0,1:T(8,128)S(1)} fusion(bf16[128,1,128,384]{3,2,1,0:T(8,128)(2,1)} %all-to-all-done, bf16[128]{0:T(256)(128)(2,1)S(1)} %convert_element_type.45, f32[]{:T(128)} %bitcast.6), kind=kOutput, calls=%fused_computation.26 | convolution fusion | flops 4838719488 | bytes 13172996 | tf_op jit(solution)/shard_map/bnrd,bnre->bde/dot_general | solution.py:31
  184.5 11.7 %custom-call.27 = f32[1,128,128]{2,1,0:T(8,128)S(1)} custom-call(f32[1,128,128]{2,1,0:T(8,128)S(1)} %cholesky.192), custom_call_target="Cholesky" | custom-call | tf_op jit(solution)/shard_map/jit(cholesky)/cholesky | solution.py:36
  196.3 9.8 %custom-call.28 = f32[1,1,128,128]{2,3,1,0:T(8,128)S(1)} custom-call(f32[1,1,128,128]{3,2,1,0:T(8,128)S(1)} %get-tuple-element.29), custom_call_target="InvertDiagBlocksLowerTriangular" | custom-call | tf_op jit(solution)/shard_map/jit(cholesky)/cholesky | solution.py:36
  206.7 11.7 %custom-call.29 = f32[1,128,128]{2,1,0:T(8,128)S(1)} custom-call(f32[1,128,128]{2,1,0:T(8,128)S(1)} %cholesky.196), custom_call_target="Cholesky" | custom-call | tf_op jit(solution)/shard_map/jit(cholesky)/cholesky | solution.py:36
  218.4 10.0 %custom-call.30 = f32[1,1,128,128]{2,3,1,0:T(8,128)S(1)} custom-call(f32[1,1,128,128]{3,2,1,0:T(8,128)S(1)} %get-tuple-element.26), custom_call_target="InvertDiagBlocksLowerTriangular" | custom-call | tf_op jit(solution)/shard_map/jit(cholesky)/cholesky | solution.py:36
  228.9 11.7 %custom-call.31 = f32[1,128,128]{2,1,0:T(8,128)S(1)} custom-call(f32[1,128,128]{2,1,0:T(8,128)S(1)} %fusion.16), custom_call_target="Cholesky" | custom-call | tf_op jit(solution)/shard_map/jit(cholesky)/cholesky | solution.py:36
  240.7 0.7 compare_reduce_fusion
  241.4 0.7 compare_reduce_fusion.1
  244.0 6.1 %while.1 = (s32[]{:T(128)}, f32[1,384,384]{2,1,0:T(8,128)S(1)}, s32[3,2]{0,1:T(2,128)S(1)}, f32[3,1,128,128]{3,2,1,0:T(8,128)S(1)}, s32[]{:T(128)}) while((s32[]{:T(128)}, f32[1,384,384]{2,1,0:T(8,128)S(1)}, s32[3,2]{0,1:T(2,128)S(1)}, f32[3,1,128,128]{3,2,1,0:T(8,128)S(1)}, s32[]{:T(128)}) %tuple.25), condition=%wide.while_cond, body=%wide.while_body.sunk | while | flops 2 | bytes 131189 | solution.py:22
  244.1 0.6 fusion.56
  244.7 1.3 bitcast_dynamic-update-slice_fusion.2
  246.2 0.6 fusion.56
  246.8 1.3 bitcast_dynamic-update-slice_fusion.2
  248.2 0.6 fusion.56
  248.8 1.3 bitcast_dynamic-update-slice_fusion.2
  250.1 29.5 %custom-call.32 = f32[1,3,128,128]{2,3,1,0:T(8,128)S(1)} custom-call(f32[1,3,128,128]{3,2,1,0:T(8,128)S(1)} %bitcast.162), custom_call_target="InvertDiagBlocksLowerTriangular" | custom-call | tf_op jit(solution)/shard_map/vmap()/triangular_solve | solution.py:22
  281.4 0.3 convolution_subtract_fusion.1
  282.0 0.4 convolution_subtract_fusion
  282.7 0.7 divide_convert_fusion
  283.5 110.9 %all-gather.2.cloned.1.call-done = bf16[128,384,256]{2,1,0:T(8,128)(2,1)} async-done(((bf16[1,384,256]{2,1,0:T(8,128)(2,1)}), bf16[128,384,256]{2,1,0:T(8,128)(2,1)}) %all-gather.2.cloned.1.call-update) | async-done | bytes 25165840 | tf_op jit(solution)/shard_map/all_gather | solution.py:56
  394.4 18.0 %convert_bitcast_fusion = bf16[128,128,256]{1,2,0:T(8,128)(2,1)} fusion(bf16[128,384,256]{2,1,0:T(8,128)(2,1)} %all-gather.2.cloned.1.call-done, bf16[128,128,384]{2,1,0:T(8,128)(2,1)} %param.4), kind=kOutput, calls=%fused_computation.6 | convolution fusion | flops 3225419776 | bytes 46137344 | tf_op jit(solution)/shard_map/bgd,bde->bge/dot_general | solution.py:53
  412.4 11.9 %copy.19 = bf16[128,128,256]{2,1,0:T(8,128)(2,1)} copy(bf16[128,128,256]{1,2,0:T(8,128)(2,1)} %convert_bitcast_fusion) | data formatting | bytes 16777216 | tf_op jit(solution)/shard_map/convert_element_type | solution.py:58
  (38 shorter events, 4.3 us)
Async XLA Ops:
  6.5 12.6 %copy-start.1 = (s32[1,128]{1,0:T(1,128)S(1)}, s32[1,128]{1,0:T(1,128)}, u32[]{:S(2)}) copy-start(s32[1,128]{1,0:T(1,128)} %param.6) | copy-start | bytes 1540
  6.5 12.8 %copy-start = (bf16[1,384,256]{2,1,0:T(8,128)(2,1)S(1)}, bf16[1,384,256]{2,1,0:T(8,128)(2,1)}, u32[]{:S(2)}) copy-start(bf16[1,384,256]{2,1,0:T(8,128)(2,1)} %param.5) | copy-start | bytes 589828
  6.5 163.5 %all-to-all-start = ((bf16[128,1,128,384]{3,2,1,0:T(8,128)(2,1)}), bf16[128,1,128,384]{3,2,1,0:T(8,128)(2,1)}, u32[]{:S(2)}, u32[]{:S(2)}) async-start(bf16[128,1,128,384]{3,2,1,0:T(8,128)(2,1)} %bitcast.154), calls=%async_computation | async-start | bytes 25165824 | tf_op jit(solution)/shard_map/all_to_all | solution.py:48
  18.4 375.9 %all-gather.2.cloned.1.call-start = ((), (), s32[]{:S(2)}) async-start(), calls=%async_computation.1 | async-start | bytes 25362432 | tf_op jit(solution)/shard_map/all_gather | solution.py:56
Sparse Core Ops, SparseCore 0:
  283.6 110.7 all-gather.1
where the time goes:
time: 432 us; the launch traced here: 431 us
  waiting for transfers between devices  262 us (61%)
  other arithmetic  87 us (20%)
  matrix products  36.1 us (8%)
  local copies, waits for them, and re-layouts  18.2 us (4%)
  between operations  16.2 us (4%)
  starting transfers between devices  11.9 us (3%)
    all_to_all x1, waiting for transfers between devices, body(): lax.all_to_all(outgoing, ('range', 'doppler'), split_axis=0, concat_axis=...  151 us
    all_gather x1, waiting for transfers between devices, body(): lax.all_gather(weights, ('range', 'doppler'), axis=0, tiled=True)  111 us
    another operation x10, other arithmetic, adapt(): factor = jnp.linalg.cholesky(covariance)  56.4 us
    another operation x3, other arithmetic, solve_one(): lax.linalg.triangular_solve(factor, inner, left_side=True, lower=True, tr...  29.5 us
    dot_general x1, matrix products, body(): jnp.einsum('bgd,bde->bge', snapshots, lax.all_gather(weights, ('range', '...  18 us
    dot_general x1, matrix products, adapt(): jnp.einsum('bnrd,bnre->bde', masked, blocks, preferred_element_type=jnp.f...  14.2 us
    convert_element_type x1, local copies, waits for them, and re-layouts, body(): return jnp.einsum('bgd,bde->bge', snapshots, lax.all_gather(weights, ('ra...  11.9 us
    all_to_all x1, starting transfers between devices, body(): lax.all_to_all(outgoing, ('range', 'doppler'), split_axis=0, concat_axis=...  11.9 us
  transfers between devices with their start and end apart: 2, of which 2 were waited for; matrix products, arithmetic and copies ran while one was open for 0% of the time, Pallas kernels for 0%

commit v1 on v0

--- a/solution.py
+++ b/solution.py
@@ -1,6 +1,8 @@
 import jax
 import jax.numpy as jnp
 from jax import lax
+from jax.experimental import pallas as pl
+from jax.experimental.pallas import tpu as pltpu
 from jax.sharding import PartitionSpec as P
 
 BLOCK = 128
@@ -17,9 +19,75 @@
     return jnp.sum(matches.astype(jnp.int32), axis=1)
 
 
-def solve_one(factor, rhs_block):
-    inner = lax.linalg.triangular_solve(factor, rhs_block, left_side=True, lower=True)
-    return lax.linalg.triangular_solve(factor, inner, left_side=True, lower=True, transpose_a=True)
+HI = lax.Precision.HIGHEST
+T = 128
+def mm(a, b, ca, cb):
+    return lax.dot_general(a, b, (((ca,), (cb,)), ((), ())), precision=HI, preferred_element_type=jnp.float32)
+
+def factor_inverse(block):
+    lane = lax.broadcasted_iota(jnp.int32, (8, T), 1)
+    sub = lax.broadcasted_iota(jnp.int32, (8, T), 0)
+    rows = [block[8 * g:8 * g + 8, :] for g in range(T // 8)]
+    for k in range(T):
+        own, off = k // 8, k % 8
+        row = rows[own][off:off + 1, :]
+        inv = 1.0 / row[:, k:k + 1]
+        scaled = jnp.where(lane[:1] == k, 1.0, row) * inv
+        for g in range(own, T // 8):
+            col = rows[g][:, k:k + 1]
+            if g == own:
+                if off == 7:
+                    continue
+                col = jnp.where(sub[:, :1] > off, col, 0.0)
+                base = jnp.where((lane == k) & (sub > off), 0.0, rows[g])
+            else:
+                base = jnp.where(lane == k, 0.0, rows[g])
+            rows[g] = base - col * scaled
+    full = jnp.concatenate(rows, axis=0)
+    i = lax.broadcasted_iota(jnp.int32, (T, T), 0)
+    j = lax.broadcasted_iota(jnp.int32, (T, T), 1)
+    pivots = jnp.sum(jnp.where(i == j, full, 0.0), axis=1, keepdims=True)
+    unit = jnp.where(i > j, full, jnp.where(i == j, 1.0, 0.0))
+    return unit * lax.rsqrt(pivots)
+
+def solve_kernel(count_ref, gram_ref, steer_ref, out_ref, cov, rhs, inv):
+    n = gram_ref.shape[0] // T
+    scale = (BLOCK * count_ref[0]).astype(jnp.float32)
+    i = lax.broadcasted_iota(jnp.int32, cov.shape, 0)
+    j = lax.broadcasted_iota(jnp.int32, cov.shape, 1)
+    cov[...] = gram_ref[...] / scale + jnp.where(i == j, LOADING, 0.0)
+    rhs[...] = steer_ref[...].astype(jnp.float32)
+    for b in range(n):
+        lo, hi = b * T, (b + 1) * T
+        inv[b] = factor_inverse(cov[lo:hi, lo:hi])
+        li = inv[b]
+        y = mm(li, rhs[lo:hi, :], 1, 0)
+        rhs[lo:hi, :] = y
+        if b + 1 < n:
+            panel = mm(cov[hi:, lo:hi], li, 1, 1)
+            cov[hi:, lo:hi] = panel
+            cov[hi:, hi:] = cov[hi:, hi:] - mm(panel, panel, 1, 1)
+            rhs[hi:, :] = rhs[hi:, :] - mm(panel, y, 1, 0)
+    for b in reversed(range(n)):
+        lo, hi = b * T, (b + 1) * T
+        y = rhs[lo:hi, :]
+        if b + 1 < n:
+            y = y - mm(cov[hi:, lo:hi], rhs[hi:, :], 0, 0)
+        rhs[lo:hi, :] = mm(inv[b], y, 0, 0)
+    solved = rhs[...]
+    response = jnp.sum(steer_ref[...].astype(jnp.float32) * solved, axis=0, keepdims=True)
+    out_ref[...] = (solved / response).astype(out_ref.dtype)
+
+def solve(count, gram, steer):
+    d, e = steer.shape
+    return pl.pallas_call(
+        solve_kernel,
+        out_shape=jax.ShapeDtypeStruct((d, e), jnp.bfloat16),
+        in_specs=[pl.BlockSpec(memory_space=pltpu.SMEM), pl.BlockSpec(memory_space=pltpu.VMEM), pl.BlockSpec(memory_space=pltpu.VMEM)],
+        out_specs=pl.BlockSpec(memory_space=pltpu.VMEM),
+        scratch_shapes=[pltpu.VMEM((d, d), jnp.float32), pltpu.VMEM((d, e), jnp.float32), pltpu.VMEM((d // T, T, T), jnp.float32)],
+        name="solve",
+    )(count, gram, steer)
 
 
 def adapt(own_snaps, train_list, train_count, steering):
@@ -29,15 +97,7 @@
     blocks = own_snaps.reshape(own_bins, block_total, gate_total // block_total, channels)
     masked = blocks * chosen.astype(own_snaps.dtype)[:, :, None, None]
     gram_sum = jnp.einsum("bnrd,bnre->bde", masked, blocks, preferred_element_type=jnp.float32)
-    scale = (BLOCK * train_count).astype(jnp.float32)
-    covariance = (
-        gram_sum / scale[:, None, None] + LOADING * jnp.eye(channels, dtype=jnp.float32)[None]
-    )
-    factor = jnp.linalg.cholesky(covariance)
-    steer_full = steering.astype(jnp.float32)
-    solved = jax.vmap(solve_one)(factor, steer_full)
-    response = jnp.sum(steer_full * solved, axis=1)
-    return (solved / response[:, None, :]).astype(jnp.bfloat16)
+    return solve(train_count, gram_sum[0], steering[0])[None]
 
 
 def body(snapshots, steering, train_list, train_count):

time: 432 us -> 372 us (0.86)
  other arithmetic: 87 us -> 0.13 us
  Pallas kernels: 0 us -> 37.4 us
  local copies, waits for them, and re-layouts: 18.2 us -> 11.9 us
    another operation x13 -> x0, other arithmetic: 86 us -> none  [the longest x10 56.4 us: adapt(): factor = jnp.linalg.cholesky(covariance)]
    pallas_call x0 -> x1, Pallas kernels: none -> 37.4 us  [solve(): pl.pallas_call(solve_kernel, out_shape=jax.ShapeDtypeStruct((d, e), jnp.b...]
    another operation x13 -> x0, local copies, waits for them, and re-layouts: 6.1 us -> none
where the time goes in v1:
time: 372 us; the launch traced here: 371 us
  waiting for transfers between devices  262 us (70%)
  Pallas kernels  37.4 us (10%)
  matrix products  33.9 us (9%)
  between operations  14.1 us (4%)
  local copies, waits for them, and re-layouts  11.9 us (3%)
  starting transfers between devices  11.9 us (3%)
    all_to_all x1, waiting for transfers between devices, body(): lax.all_to_all(outgoing, ('range', 'doppler'), split_axis=0, concat_axis=...  151 us
    all_gather x1, waiting for transfers between devices, body(): lax.all_gather(weights, ('range', 'doppler'), axis=0, tiled=True)  111 us
    pallas_call x1, Pallas kernels, solve(): pl.pallas_call(solve_kernel, out_shape=jax.ShapeDtypeStruct((d, e), jnp.b...  37.4 us
    dot_general x1, matrix products, body(): jnp.einsum('bgd,bde->bge', snapshots, lax.all_gather(weights, ('range', '...  18 us
    dot_general x1, matrix products, adapt(): jnp.einsum('bnrd,bnre->bde', masked, blocks, preferred_element_type=jnp.f...  16 us
    convert_element_type x1, local copies, waits for them, and re-layouts, body(): return jnp.einsum('bgd,bde->bge', snapshots, lax.all_gather(weights, ('ra...  11.9 us
    all_to_all x1, starting transfers between devices, body(): lax.all_to_all(outgoing, ('range', 'doppler'), split_axis=0, concat_axis=...  11.9 us
  transfers between devices with their start and end apart: 2, of which 2 were waited for; matrix products, arithmetic and copies ran while one was open for 0% of the time, Pallas kernels for 0%

profile of v1, /device:TPU:1, one launch (start us, length us, event | category | flops | bytes accessed | tf_op | source)
XLA Modules:
  0.0 371.1 jit_solution(1470413657331888708)
XLA Ops:
  6.5 0.0 copy-start
  6.5 11.9 %all-to-all-start = ((bf16[128,1,128,384]{3,2,1,0:T(8,128)(2,1)}), bf16[128,1,128,384]{3,2,1,0:T(8,128)(2,1)}, u32[]{:S(2)}, u32[]{:S(2)}) async-start(bf16[128,1,128,384]{3,2,1,0:T(8,128)(2,1)} %bitcast.22), calls=%async_computation | async-start | bytes 25165824 | tf_op jit(solution)/shard_map/all_to_all | solution.py:108
  18.4 0.0 all-gather.3.cloned.1.call-start
  19.2 0.0 copy-done
  19.2 0.1 convert_reduce_fusion
  19.3 150.7 %all-to-all-done = bf16[128,1,128,384]{3,2,1,0:T(8,128)(2,1)} async-done(((bf16[128,1,128,384]{3,2,1,0:T(8,128)(2,1)}), bf16[128,1,128,384]{3,2,1,0:T(8,128)(2,1)}, u32[]{:S(2)}, u32[]{:S(2)}) %all-to-all-start) | async-done | bytes 12582944 | tf_op jit(solution)/shard_map/all_to_all | solution.py:108
  170.0 16.0 %fusion.5.gram_ref = f32[384,384]{1,0:T(8,128)} fusion(bf16[128,1,128,384]{3,2,1,0:T(8,128)(2,1)} %all-to-all-done, bf16[128]{0:T(256)(128)(2,1)S(1)} %convert_element_type.27), kind=kOutput, calls=%fused_computation.6 | convolution fusion | flops 4838129664 | bytes 13172992 | tf_op jit(solution)/shard_map/bnrd,bnre->bde/dot_general | solution.py:99
  186.0 37.4 %solve.1 = bf16[384,256]{1,0:T(8,128)(2,1)} custom-call(s32[1]{0:T(128)} %copy.16.count_ref, f32[384,384]{1,0:T(8,128)} %fusion.5.gram_ref, bf16[384,256]{1,0:T(8,128)(2,1)} %bitcast.24), custom_call_target="tpu_custom_call" | custom-call | tf_op jit(solution)/shard_map/solve/pallas_call | solution.py:83
  223.4 0.0 all-gather.3.cloned.1.call-update
  223.4 110.9 %all-gather.3.cloned.1.call-done = bf16[49152,256]{1,0:T(8,128)(2,1)} async-done(((bf16[384,256]{1,0:T(8,128)(2,1)}), bf16[49152,256]{1,0:T(8,128)(2,1)}) %all-gather.3.cloned.1.call-update) | async-done | bytes 25165840 | tf_op jit(solution)/shard_map/all_gather | solution.py:116
  334.3 18.0 %convert_bitcast_fusion = bf16[128,128,256]{1,2,0:T(8,128)(2,1)} fusion(bf16[128,384,256]{2,1,0:T(8,128)(2,1)} %bitcast.23, bf16[128,128,384]{2,1,0:T(8,128)(2,1)} %param.4), kind=kOutput, calls=%fused_computation.4 | convolution fusion | flops 3225419776 | bytes 46137344 | tf_op jit(solution)/shard_map/bgd,bde->bge/dot_general | solution.py:113
  352.3 11.9 %copy.13 = bf16[128,128,256]{2,1,0:T(8,128)(2,1)} copy(bf16[128,128,256]{1,2,0:T(8,128)(2,1)} %convert_bitcast_fusion) | data formatting | bytes 16777216 | tf_op jit(solution)/shard_map/convert_element_type | solution.py:118
  (2 shorter events, 0.0 us)
Async XLA Ops:
  6.5 12.6 %copy-start = (s32[1,128]{1,0:T(1,128)S(1)}, s32[1,128]{1,0:T(1,128)}, u32[]{:S(2)}) copy-start(s32[1,128]{1,0:T(1,128)} %param.6) | copy-start | bytes 1540
  6.5 163.5 %all-to-all-start = ((bf16[128,1,128,384]{3,2,1,0:T(8,128)(2,1)}), bf16[128,1,128,384]{3,2,1,0:T(8,128)(2,1)}, u32[]{:S(2)}, u32[]{:S(2)}) async-start(bf16[128,1,128,384]{3,2,1,0:T(8,128)(2,1)} %bitcast.22), calls=%async_computation | async-start | bytes 25165824 | tf_op jit(solution)/shard_map/all_to_all | solution.py:108
  18.4 315.9 %all-gather.3.cloned.1.call-start = ((), (), s32[]{:S(2)}) async-start(), calls=%async_computation.1 | async-start | bytes 25362432 | tf_op jit(solution)/shard_map/all_gather | solution.py:116
Sparse Core Ops, SparseCore 0:
  223.6 110.7 all-gather.2

commit v2 on v1

--- a/solution.py
+++ b/solution.py
@@ -90,6 +90,132 @@
     )(count, gram, steer)
 
 
+MESH = pl.DeviceIdType.MESH
+SIDE = 4
+ORDERS = (("x", "y", "z"), ("y", "z", "x"), ("z", "x", "y"))
+
+def place():
+    r, d = lax.axis_index("range"), lax.axis_index("doppler")
+    return {"z": r // SIDE, "y": r % SIDE, "x": d // 2, "c": d % 2}
+
+def device(at):
+    return (at["z"] * SIDE + at["y"], at["x"] * 2 + at["c"])
+
+def moved(at, axis, step):
+    return {**at, axis: (at[axis] + step) % SIDE}
+
+def twin(at):
+    return {**at, "c": 1 - at["c"]}
+
+def greet(at):
+    barrier = pltpu.get_barrier_semaphore()
+    friends = [moved(at, a, s) for a in "xyz" for s in (1, SIDE - 1)] + [twin(at)]
+    for friend in friends:
+        pl.semaphore_signal(barrier, inc=1, device_id=device(friend), device_id_type=MESH)
+    pl.semaphore_wait(barrier, len(friends))
+
+def gather_kernel(own_ref, all_ref, local_sem, send_sem, recv_sem, twin_send, twin_recv):
+    at = place()
+    rows = own_ref.shape[0] // 3
+    half = rows // 2
+    greet(at)
+
+    def window(part, gathered, where, halves):
+        lo, count = (part * rows, rows) if halves is None else (part * rows + halves * half, half)
+        pick = tuple(slice(None) if a in gathered else where[a] for a in "zyx")
+        return all_ref.at[pick + (where["c"], pl.ds(lo, count), slice(None))]
+
+    pending = []
+    def send(part, stage, kind, gathered, where, halves, target):
+        ref = window(part, gathered, where, halves)
+        copy = pltpu.make_async_remote_copy(
+            src_ref=ref, dst_ref=ref, send_sem=send_sem.at[part, stage, kind], recv_sem=recv_sem.at[part, stage, kind],
+            device_id=device(target), device_id_type=MESH)
+        copy.start()
+        pending.append(copy)
+    def arrive(part, stage, kind, gathered, where, halves):
+        ref = window(part, gathered, where, halves)
+        pltpu.make_async_remote_copy(
+            src_ref=ref, dst_ref=ref, send_sem=send_sem.at[part, stage, kind], recv_sem=recv_sem.at[part, stage, kind],
+            device_id=device(at), device_id_type=MESH).wait_recv()
+    shared = []
+    def share(part, stage, kind, gathered, where, halves):
+        ref = window(part, gathered, where, halves)
+        copy = pltpu.make_async_remote_copy(
+            src_ref=ref, dst_ref=ref, send_sem=twin_send.at[part, stage, kind], recv_sem=twin_recv.at[part, stage, kind],
+            device_id=device(twin(at)), device_id_type=MESH)
+        copy.start()
+        shared.append((copy, part, stage, kind, gathered, where, halves))
+
+    mine = all_ref.at[at["z"], at["y"], at["x"], at["c"]]
+    copy = pltpu.make_async_copy(own_ref, mine, local_sem)
+    copy.start()
+    copy.wait()
+    for part in range(3):
+        share(part, 3, 0, (), at, None)
+    for stage in range(3):
+        for part in range(3):
+            axis, gathered = ORDERS[part][stage], ORDERS[part][:stage]
+            up, down = moved(at, axis, 1), moved(at, axis, SIDE - 1)
+            send(part, stage, 0, gathered, at, 0, up)
+            send(part, stage, 1, gathered, at, 1, down)
+            send(part, stage, 2, gathered, at, 1, up)
+            send(part, stage, 3, gathered, at, 0, down)
+        for part in range(3):
+            axis, gathered = ORDERS[part][stage], ORDERS[part][:stage]
+            up, down = moved(at, axis, 1), moved(at, axis, SIDE - 1)
+            arrive(part, stage, 0, gathered, down, 0)
+            send(part, stage, 4, gathered, down, 0, up)
+            share(part, stage, 0, gathered, down, 0)
+            arrive(part, stage, 1, gathered, up, 1)
+            send(part, stage, 5, gathered, up, 1, down)
+            share(part, stage, 1, gathered, up, 1)
+        for part in range(3):
+            axis, gathered = ORDERS[part][stage], ORDERS[part][:stage]
+            up, down, far = moved(at, axis, 1), moved(at, axis, SIDE - 1), moved(at, axis, 2)
+            for kind, where, halves in ((2, down, 1), (3, up, 0), (4, far, 0), (5, far, 1)):
+                arrive(part, stage, kind, gathered, where, halves)
+                share(part, stage, kind, gathered, where, halves)
+    for copy in pending:
+        copy.wait_send()
+    for copy, part, stage, kind, gathered, where, halves in shared:
+        copy.wait_send()
+        ref = window(part, gathered, twin(where), halves)
+        pltpu.make_async_remote_copy(
+            src_ref=ref, dst_ref=ref, send_sem=twin_send.at[part, stage, kind], recv_sem=twin_recv.at[part, stage, kind],
+            device_id=device(twin(at)), device_id_type=MESH).wait_recv()
+
+def gather(own):
+    rows, columns = own.shape
+    whole = pl.pallas_call(
+        gather_kernel,
+        out_shape=jax.ShapeDtypeStruct((SIDE, SIDE, SIDE, 2, rows, columns), own.dtype),
+        in_specs=[pl.BlockSpec(memory_space=pltpu.VMEM)],
+        out_specs=pl.BlockSpec(memory_space=pl.ANY),
+        scratch_shapes=[pltpu.SemaphoreType.DMA, pltpu.SemaphoreType.DMA((3, 3, 6)), pltpu.SemaphoreType.DMA((3, 3, 6)),
+                        pltpu.SemaphoreType.DMA((3, 4, 6)), pltpu.SemaphoreType.DMA((3, 4, 6))],
+        compiler_params=pltpu.CompilerParams(collective_id=1, has_side_effects=True),
+        name="gather",
+    )(own)
+    return whole.reshape(SIDE * SIDE * SIDE * 2, rows, columns)
+
+def apply_kernel(snap_ref, weight_ref, out_ref):
+    for b in range(snap_ref.shape[0]):
+        out_ref[b] = jnp.dot(snap_ref[b], weight_ref[b], preferred_element_type=jnp.float32).astype(out_ref.dtype)
+
+def beams(snapshots, weights, step=8):
+    bins, gates, channels = snapshots.shape
+    looks = weights.shape[2]
+    return pl.pallas_call(
+        apply_kernel,
+        grid=(bins // step,),
+        out_shape=jax.ShapeDtypeStruct((bins, gates, looks), jnp.bfloat16),
+        in_specs=[pl.BlockSpec((step, gates, channels), lambda i: (i, 0, 0)), pl.BlockSpec((step, channels, looks), lambda i: (i, 0, 0))],
+        out_specs=pl.BlockSpec((step, gates, looks), lambda i: (i, 0, 0)),
+        name="beams",
+    )(snapshots, weights)
+
+
 def adapt(own_snaps, train_list, train_count, steering):
     own_bins, gate_total, channels = own_snaps.shape
     block_total = train_list.shape[1]
@@ -110,12 +236,7 @@
     )
     own_snaps = jnp.moveaxis(arrived, 1, 0).reshape(own_bins, devices * gate_rows, channels)
     weights = adapt(own_snaps, train_list, train_count, steering)
-    return jnp.einsum(
-        "bgd,bde->bge",
-        snapshots,
-        lax.all_gather(weights, ("range", "doppler"), axis=0, tiled=True),
-        preferred_element_type=jnp.float32,
-    ).astype(jnp.bfloat16)
+    return beams(snapshots, gather(weights[0]))
 
 
 def solution(mesh):

time: 372 us -> 324 us (0.87)
  waiting for transfers between devices: 262 us -> 151 us
  Pallas kernels: 37.4 us -> 144 us
  matrix products: 33.9 us -> 15.9 us
  between operations: 14.1 us -> 0.68 us
  local copies, waits for them, and re-layouts: 11.9 us -> 0.01 us
    all_gather x1 -> x0, waiting for transfers between devices: 111 us -> none  [body(): lax.all_gather(weights, ('range', 'doppler'), axis=0, tiled=True)]
    pallas_call x0 -> x2, Pallas kernels: none -> 107 us  [the longest x1 85.4 us: gather(): pl.pallas_call(gather_kernel, out_shape=jax.ShapeDtypeStruct((SIDE, SIDE,...]
    dot_general x1 -> x0, matrix products: 18 us -> none  [body(): jnp.einsum('bgd,bde->bge', snapshots, lax.all_gather(weights, ('range', '...]
    convert_element_type x1 -> x0, local copies, waits for them, and re-layouts: 11.9 us -> none  [body(): return jnp.einsum('bgd,bde->bge', snapshots, lax.all_gather(weights, ('ra...]
  transfers between devices with their start and end apart: 2 -> 1, of which waited for: 2 -> 1; matrix products, arithmetic and copies ran while one was open for 0% -> 0% of each run, Pallas kernels for 0% -> 0%
where the time goes in v2:
time: 324 us
  waiting for transfers between devices  151 us (47%)
  Pallas kernels  144 us (44%)
  matrix products  15.9 us (5%)
  starting transfers between devices  11.9 us (4%)
    all_to_all x1, waiting for transfers between devices, body(): lax.all_to_all(outgoing, ('range', 'doppler'), split_axis=0, concat_axis=...  151 us
    pallas_call x1, Pallas kernels, gather(): pl.pallas_call(gather_kernel, out_shape=jax.ShapeDtypeStruct((SIDE, SIDE,...  85.4 us
    pallas_call x1, Pallas kernels, solve(): pl.pallas_call(solve_kernel, out_shape=jax.ShapeDtypeStruct((d, e), jnp.b...  37.4 us
    pallas_call x1, Pallas kernels, beams(): pl.pallas_call(apply_kernel, grid=(bins // step,), out_shape=jax.ShapeDty...  21.4 us
    dot_general x1, matrix products, adapt(): jnp.einsum('bnrd,bnre->bde', masked, blocks, preferred_element_type=jnp.f...  15.9 us
    all_to_all x1, starting transfers between devices, body(): lax.all_to_all(outgoing, ('range', 'doppler'), split_axis=0, concat_axis=...  11.9 us
  transfers between devices with their start and end apart: 1, of which 1 were waited for; matrix products, arithmetic and copies ran while one was open for 0% of the time, Pallas kernels for 0%

profile of v2, /device:TPU:1, one launch (start us, length us, event | category | flops | bytes accessed | tf_op | source)
XLA Modules:
  0.0 323.7 jit_solution(5574948792296676691)
XLA Ops:
  0.0 0.0 copy-start
  0.0 11.9 %all-to-all-start = ((bf16[128,1,128,384]{3,2,1,0:T(8,128)(2,1)}), bf16[128,1,128,384]{3,2,1,0:T(8,128)(2,1)}, u32[]{:S(2)}, u32[]{:S(2)}) async-start(bf16[128,1,128,384]{3,2,1,0:T(8,128)(2,1)} %bitcast.19), calls=%async_computation | async-start | bytes 25165824 | tf_op jit(solution)/shard_map/all_to_all | solution.py:234
  12.6 0.0 copy-done
  12.6 0.1 convert_reduce_fusion
  12.7 150.8 %all-to-all-done = bf16[128,1,128,384]{3,2,1,0:T(8,128)(2,1)} async-done(((bf16[128,1,128,384]{3,2,1,0:T(8,128)(2,1)}), bf16[128,1,128,384]{3,2,1,0:T(8,128)(2,1)}, u32[]{:S(2)}, u32[]{:S(2)}) %all-to-all-start) | async-done | bytes 12582944 | tf_op jit(solution)/shard_map/all_to_all | solution.py:234
  163.5 15.9 %fusion.5.gram_ref = f32[384,384]{1,0:T(8,128)} fusion(bf16[128,1,128,384]{3,2,1,0:T(8,128)(2,1)} %all-to-all-done, bf16[128]{0:T(256)(128)(2,1)S(1)} %convert_element_type.21), kind=kOutput, calls=%fused_computation.5 | convolution fusion | flops 4838129664 | bytes 13172992 | tf_op jit(solution)/shard_map/bnrd,bnre->bde/dot_general | solution.py:225
  179.4 37.4 %solve.1.own_ref = bf16[384,256]{1,0:T(8,128)(2,1)} custom-call(s32[1]{0:T(128)} %copy.9.count_ref, f32[384,384]{1,0:T(8,128)} %fusion.5.gram_ref, bf16[384,256]{1,0:T(8,128)(2,1)} %bitcast.20), custom_call_target="tpu_custom_call" | custom-call | tf_op jit(solution)/shard_map/solve/pallas_call | solution.py:83
  216.9 85.4 %gather.1 = bf16[4,4,4,2,384,256]{5,4,3,2,1,0:T(8,128)(2,1)} custom-call(bf16[384,256]{1,0:T(8,128)(2,1)} %solve.1.own_ref), custom_call_target="tpu_custom_call" | custom-call | tf_op jit(solution)/shard_map/gather/pallas_call | solution.py:190
  302.3 21.4 %beams.1 = bf16[128,128,256]{2,1,0:T(8,128)(2,1)} custom-call(bf16[128,128,384]{2,1,0:T(8,128)(2,1)} %snap_ref.1, bf16[128,384,256]{2,1,0:T(8,128)(2,1)} %bitcast.18), custom_call_target="tpu_custom_call" | custom-call | tf_op jit(solution)/shard_map/beams/pallas_call | solution.py:209
  (2 shorter events, 0.0 us)
Async XLA Ops:
  0.0 12.6 %copy-start = (s32[1,128]{1,0:T(1,128)S(1)}, s32[1,128]{1,0:T(1,128)}, u32[]{:S(2)}) copy-start(s32[1,128]{1,0:T(1,128)} %param.6) | copy-start | bytes 1540
  0.0 163.5 %all-to-all-start = ((bf16[128,1,128,384]{3,2,1,0:T(8,128)(2,1)}), bf16[128,1,128,384]{3,2,1,0:T(8,128)(2,1)}, u32[]{:S(2)}, u32[]{:S(2)}) async-start(bf16[128,1,128,384]{3,2,1,0:T(8,128)(2,1)} %bitcast.19), calls=%async_computation | async-start | bytes 25165824 | tf_op jit(solution)/shard_map/all_to_all | solution.py:234

commit v3 on v2

--- a/solution.py
+++ b/solution.py
@@ -6,8 +6,6 @@
 from jax.sharding import PartitionSpec as P
 
 BLOCK = 128
-
-
 LOADING = 0.1
 
 
@@ -51,11 +49,15 @@
     return unit * lax.rsqrt(pivots)
 
 def solve_kernel(count_ref, gram_ref, steer_ref, out_ref, cov, rhs, inv):
-    n = gram_ref.shape[0] // T
+    n = cov.shape[0] // T
     scale = (BLOCK * count_ref[0]).astype(jnp.float32)
-    i = lax.broadcasted_iota(jnp.int32, cov.shape, 0)
-    j = lax.broadcasted_iota(jnp.int32, cov.shape, 1)
-    cov[...] = gram_ref[...] / scale + jnp.where(i == j, LOADING, 0.0)
+    i = lax.broadcasted_iota(jnp.int32, (T, T), 0)
+    j = lax.broadcasted_iota(jnp.int32, (T, T), 1)
+    tiles = unpack(gram_ref, pltpu.roll)
+    for (r, c), tile in zip(((0, 0), (1, 0), (1, 1), (2, 0), (2, 1), (2, 2)), tiles):
+        tile = tile / scale
+        cov[r * T:(r + 1) * T, c * T:(c + 1) * T] = tile + jnp.where(i == j, LOADING, 0.0) if r == c else tile
+    cov[T:2 * T, 2 * T:] = jnp.zeros((T, T), jnp.float32)
     rhs[...] = steer_ref[...].astype(jnp.float32)
     for b in range(n):
         lo, hi = b * T, (b + 1) * T
@@ -216,27 +218,262 @@
     )(snapshots, weights)
 
 
-def adapt(own_snaps, train_list, train_count, steering):
-    own_bins, gate_total, channels = own_snaps.shape
-    block_total = train_list.shape[1]
-    chosen = selection(train_list, train_count)
-    blocks = own_snaps.reshape(own_bins, block_total, gate_total // block_total, channels)
-    masked = blocks * chosen.astype(own_snaps.dtype)[:, :, None, None]
-    gram_sum = jnp.einsum("bnrd,bnre->bde", masked, blocks, preferred_element_type=jnp.float32)
-    return solve(train_count, gram_sum[0], steering[0])[None]
+HALF = 64
+PACKED = 200
+CUT = 104
+TOP, LOW, ALL = (0, CUT), (CUT, PACKED - CUT), (0, PACKED)
+REDUCE = (("z", "y", "x"), ("x", "z", "y"), ("y", "x", "z"))
+
+def cross(a, b):
+    return lax.dot_general(a, b, (((0,), (0,)), ((), ())), preferred_element_type=jnp.float32)
+
+def packed_part(part, snaps):
+    first, second, third = snaps[:, :T], snaps[:, T:2 * T], snaps[:, 2 * T:]
+    i = lax.broadcasted_iota(jnp.int32, (HALF, T), 0)
+    j = lax.broadcasted_iota(jnp.int32, (HALF, T), 1)
+    if part == 2:
+        both = cross(third, jnp.concatenate([first, third], axis=1))
+        tile, square = both[:, :T], both[:, T:]
+        turned = pltpu.roll(square[:HALF], HALF, axis=1)
+        fold = jnp.where(j - HALF > i, turned, square[HALF:])
+        ridge = jnp.where(j - HALF == i, turned, 0.0)
+    else:
+        lo = part * HALF
+        lower = cross(first, first)[lo:lo + HALF]
+        if part == 0:
+            both = cross(second, snaps[:, :2 * T])
+            tile, upper = both[:, :T], both[lo:lo + HALF, T:]
+        else:
+            both = cross(second, snaps[:, T:])
+            tile, upper = both[:, T:], both[lo:lo + HALF, :T]
+        fold = jnp.where(j <= i + lo, lower, upper)
+        ridge = jnp.where(j == i + lo, upper, 0.0)
+    return tile, fold, jnp.broadcast_to(jnp.sum(ridge, axis=0, keepdims=True), (8, T))
+
+def unpack(packed, roll):
+    i = lax.broadcasted_iota(jnp.int32, (T, T), 0)
+    j = lax.broadcasted_iota(jnp.int32, (T, T), 1)
+    fold = jnp.concatenate([packed[0, T:T + HALF], packed[1, T:T + HALF]], axis=0)
+    ridge = packed[0, PACKED - 8:PACKED - 7] + packed[1, PACKED - 8:PACKED - 7]
+    t00 = jnp.where(j <= i, fold, fold.T)
+    t11 = jnp.where(j > i, fold, jnp.where(i == j, ridge, fold.T))
+    low = packed[2, T:T + HALF]
+    mixed = jnp.concatenate([roll(low, HALF, 1), low], axis=0)
+    ridge = roll(packed[2, PACKED - 8:], HALF, 1)[:1]
+    keep = ((i < HALF) & (j < HALF) & (j > i)) | ((i >= HALF) & (j <= i))
+    t22 = jnp.where((i == j) & (i < HALF), ridge, jnp.where(keep, mixed, mixed.T))
+    return t00, packed[0, :T], t11, packed[2, :T], packed[1, :T].T, t22
+
+def reduce_kernel(snap_ref, chosen_ref, out_ref, own, other, marks, grams, far1, down1, up1, far2, down2, up2, far3, down3, up3,
+                  own_sem, twin_send, twin_recv, mark_send, mark_recv, send1, recv1, send2, recv2):
+    at = place()
+    greet(at)
+    twin_at = twin(at)
+    me = ((at["z"] * SIDE + at["y"]) * SIDE + at["x"]) * 2
+    far = (far1, far2, far3)
+    down_in = (down1, down2, down3)
+    up_in = (up1, up2, up3)
+
+    def turn(axis, step):
+        return (at[axis] + step) % SIDE
+
+    def own_copy(z):
+        return pltpu.make_async_copy(snap_ref.at[z, :, :, at["c"]], own.at[z], own_sem.at[z])
+    def twin_copy(z):
+        return pltpu.make_async_remote_copy(
+            src_ref=snap_ref.at[z, :, :, twin_at["c"]], dst_ref=other.at[z], send_sem=twin_send.at[z], recv_sem=twin_recv.at[z],
+            device_id=device(twin_at), device_id_type=MESH)
+    order = [turn("z", s) for s in (2, 1, 3, 0)]
+
+    def mark_copy(stage, kind):
+        axis = "xyz"[stage]
+        where = moved(at, axis, SIDE - 1) if kind == 2 else at
+        ref = marks.at[(where["z"], where["y"], where["x"])[:SIDE - 1 - stage]]
+        target = moved(at, axis, SIDE - 1 if kind == 1 else 1)
+        return pltpu.make_async_remote_copy(
+            src_ref=ref, dst_ref=ref, send_sem=mark_send.at[stage, kind], recv_sem=mark_recv.at[stage, kind],
+            device_id=device(target), device_id_type=MESH)
+    for z in order:
+        twin_copy(z).start()
+        own_copy(z).start()
+    marks[at["z"], at["y"], at["x"]] = chosen_ref[...]
+    for stage in range(3):
+        mark_copy(stage, 0).start()
+        mark_copy(stage, 1).start()
+        mark_copy(stage, 0).wait_recv()
+        mark_copy(stage, 2).start()
+        mark_copy(stage, 1).wait_recv()
+        mark_copy(stage, 2).wait_recv()
+    for stage in range(3):
+        for kind in range(3):
+            mark_copy(stage, kind).wait_send()
+
+    lane = lax.broadcasted_iota(jnp.int32, (1, T), 1)
+    def ready(z):
+        own_copy(z).wait()
+        twin_copy(z).wait_recv()
+        def mask(n, carry):
+            y, x = n // SIDE, n % SIDE
+            row = marks[z, y, x][:1]
+            for ref, block in ((own, me + at["c"]), (other, me + twin_at["c"])):
+                keep = jnp.sum(jnp.where(lane == block, row, 0.0), axis=1, keepdims=True)
+                ref[z, y, x] = (ref[z, y, x].astype(jnp.float32) * keep).astype(jnp.bfloat16)
+            return carry
+        lax.fori_loop(0, SIDE * SIDE, mask, 0)
+
+    def compute(part, i3, i2):
+        names = REDUCE[part]
+        def one(i1, carry):
+            where = dict(zip(names, (i3, i2, i1)))
+            spot = (where["z"], where["y"], where["x"])
+            snaps = jnp.concatenate([own[spot], other[spot]], axis=0)
+            tile, fold, ridge = packed_part(part, snaps)
+            grams[part, i3, i2, i1, 0:T] = tile
+            grams[part, i3, i2, i1, T:T + HALF] = fold
+            grams[part, i3, i2, i1, T + HALF:PACKED] = ridge
+            return carry
+        lax.fori_loop(0, SIDE, one, 0)
+
+    KIND = (
+        (2, TOP, "far", 1), (2, LOW, "far", SIDE - 1), (1, LOW, "near", 1),
+        (SIDE - 1, TOP, "near", SIDE - 1), (1, TOP, "near", 1), (SIDE - 1, LOW, "near", SIDE - 1),
+    )
+    def hop(part, stage, kind, chunk=None):
+        step, (lo, count), slot, way = KIND[kind]
+        names = REDUCE[part]
+        prefix = tuple(at[a] for a in names[:stage])
+        tail = () if chunk is None else (chunk,)
+        rows = (slice(None),) * (2 - stage - len(tail)) + (pl.ds(lo, count), slice(None))
+        src = grams.at[(part,) + prefix + (turn(names[stage], step),) + tail + rows]
+        box = far[stage] if slot == "far" else (down_in[stage] if way == 1 else up_in[stage])
+        dst = box.at[(part,) + tail + rows]
+        if chunk is None:
+            ss, rs = send2.at[part, stage - 1, kind], recv2.at[part, stage - 1, kind]
+        else:
+            ss, rs = send1.at[part, kind, chunk], recv1.at[part, kind, chunk]
+        return pltpu.make_async_remote_copy(
+            src_ref=src, dst_ref=dst, send_sem=ss, recv_sem=rs,
+            device_id=device(moved(at, names[stage], way)), device_id_type=MESH)
+
+    def add_far(part, stage, kind, chunk=None):
+        names = REDUCE[part]
+        prefix = tuple(at[a] for a in names[:stage])
+        tail = () if chunk is None else (chunk,)
+        step, (lo, count) = (1, TOP) if kind == 0 else (SIDE - 1, LOW)
+        whole = (slice(None),) * (2 - stage - len(tail)) + (slice(lo, lo + count), slice(None))
+        spot = (part,) + prefix + (turn(names[stage], step),) + tail + whole
+        grams[spot] = grams[spot] + far[stage][(part,) + tail + whole]
+
+    def add_near(part, stage, chunk=None):
+        names = REDUCE[part]
+        tail = () if chunk is None else (chunk,)
+        spot = (part,) + tuple(at[a] for a in names[:stage + 1]) + tail
+        got = (part,) + tail
+        grams[spot] = grams[spot] + down_in[stage][got] + up_in[stage][got]
+
+    def second(part, q):
+        return (at[REDUCE[part][1]] + 6 - q) % SIDE
+
+    def loop(body):
+        def run(q, carry):
+            body(q)
+            return carry
+        lax.fori_loop(0, SIDE, run, 0)
+
+    def far_out(part):
+        def body(q):
+            compute(part, turn(REDUCE[part][0], 2), second(part, q))
+            hop(part, 0, 0, second(part, q)).start()
+            hop(part, 0, 1, second(part, q)).start()
+        loop(body)
+
+    ready(order[0])
+    far_out(0)
+    for z in order[1:]:
+        ready(z)
+    far_out(1)
+    far_out(2)
+
+    def near_out(q):
+        for part in range(3):
+            for step, kind in ((1, 2), (SIDE - 1, 3)):
+                compute(part, turn(REDUCE[part][0], step), second(part, q))
+                hop(part, 0, kind, second(part, q)).start()
+    loop(near_out)
+
+    def relay(q):
+        for part in range(3):
+            compute(part, at[REDUCE[part][0]], second(part, q))
+        for part in range(3):
+            chunk = second(part, q)
+            for kind in (0, 1):
+                hop(part, 0, kind, chunk).wait_recv()
+                add_far(part, 0, kind, chunk)
+                hop(part, 0, kind + 4, chunk).start()
+    loop(relay)
+
+    for q in range(SIDE):
+        for part in range(3):
+            chunk = second(part, q)
+            for kind in (2, 3, 4, 5):
+                hop(part, 0, kind, chunk).wait_recv()
+            add_near(part, 0, chunk)
+            for kind in ((0, 1), (2,), (), (3,))[q]:
+                hop(part, 1, kind).start()
+    for stage in (1, 2):
+        for part in range(3):
+            for kind in (0, 1):
+                hop(part, stage, kind).wait_recv()
+                add_far(part, stage, kind)
+                hop(part, stage, kind + 4).start()
+        for part in range(3):
+            for kind in (2, 3, 4, 5):
+                hop(part, stage, kind).wait_recv()
+            add_near(part, stage)
+            if stage == 1:
+                for kind in range(4):
+                    hop(part, 2, kind).start()
+    for part in range(3):
+        out_ref[part] = grams[(part,) + tuple(at[a] for a in REDUCE[part])]
+
+    for z in order:
+        twin_copy(z).wait_send()
+    def drain(q):
+        for part in range(3):
+            for kind in range(6):
+                hop(part, 0, kind, q).wait_send()
+    loop(drain)
+    for part in range(3):
+        for stage in (1, 2):
+            for kind in range(6):
+                hop(part, stage, kind).wait_send()
+
+def reduce_grams(snapshots, chosen):
+    bins, gates, channels = snapshots.shape
+    split = snapshots.reshape(SIDE, SIDE, SIDE, 2, gates, channels)
+    f32, sem = jnp.float32, pltpu.SemaphoreType.DMA
+    boxes = [pltpu.VMEM((3,) + (SIDE,) * n + (PACKED, T), f32) for n in (2, 2, 2, 1, 1, 1, 0, 0, 0)]
+    return pl.pallas_call(
+        reduce_kernel,
+        out_shape=jax.ShapeDtypeStruct((3, PACKED, T), f32),
+        in_specs=[pl.BlockSpec(memory_space=pl.ANY), pl.BlockSpec(memory_space=pltpu.VMEM)],
+        out_specs=pl.BlockSpec(memory_space=pltpu.VMEM),
+        scratch_shapes=[
+            pltpu.VMEM((SIDE, SIDE, SIDE, gates, channels), jnp.bfloat16), pltpu.VMEM((SIDE, SIDE, SIDE, gates, channels), jnp.bfloat16),
+            pltpu.VMEM((SIDE, SIDE, SIDE, 8, T), f32), pltpu.VMEM((3, SIDE, SIDE, SIDE, PACKED, T), f32), *boxes,
+            sem((SIDE,)), sem((SIDE,)), sem((SIDE,)), sem((3, 3)), sem((3, 3)),
+            sem((3, 6, SIDE)), sem((3, 6, SIDE)), sem((3, 2, 6)), sem((3, 2, 6)),
+        ],
+        compiler_params=pltpu.CompilerParams(collective_id=2, has_side_effects=True, vmem_limit_bytes=67000000),
+        name="reduce_grams",
+    )(split, chosen)
 
 
 def body(snapshots, steering, train_list, train_count):
-    bin_total, gate_rows, channels = snapshots.shape
-    own_bins = steering.shape[0]
-    devices = bin_total // own_bins
-    outgoing = snapshots.reshape(devices, own_bins, gate_rows, channels)
-    arrived = lax.all_to_all(
-        outgoing, ("range", "doppler"), split_axis=0, concat_axis=0, tiled=True
-    )
-    own_snaps = jnp.moveaxis(arrived, 1, 0).reshape(own_bins, devices * gate_rows, channels)
-    weights = adapt(own_snaps, train_list, train_count, steering)
-    return beams(snapshots, gather(weights[0]))
+    chosen = selection(train_list, train_count).astype(jnp.float32)
+    packed = reduce_grams(snapshots, jnp.broadcast_to(chosen, (8, BLOCK)))
+    weights = solve(train_count, packed, steering[0])
+    return beams(snapshots, gather(weights))
 
 
 def solution(mesh):

time: 324 us -> 246 us (0.76)
  waiting for transfers between devices: 151 us -> 0 us
  Pallas kernels: 144 us -> 244 us
  matrix products: 15.9 us -> 0 us
  starting transfers between devices: 11.9 us -> 0 us
    all_to_all x1 -> x0, waiting for transfers between devices: 151 us -> none  [body(): lax.all_to_all(outgoing, ('range', 'doppler'), split_axis=0, concat_axis=...]
    pallas_call x0 -> x1, Pallas kernels: none -> 110 us  [reduce_grams(): pl.pallas_call(reduce_kernel, out_shape=jax.ShapeDtypeStruct((3, PACKED,...]
    dot_general x1 -> x0, matrix products: 15.9 us -> none  [adapt(): jnp.einsum('bnrd,bnre->bde', masked, blocks, preferred_element_type=jnp.f...]
    all_to_all x1 -> x0, starting transfers between devices: 11.9 us -> none  [body(): lax.all_to_all(outgoing, ('range', 'doppler'), split_axis=0, concat_axis=...]
    pallas_call x1, Pallas kernels: 85.4 us -> 75.1 us  [gather(): pl.pallas_call(gather_kernel, out_shape=jax.ShapeDtypeStruct((SIDE, SIDE,...]
  transfers between devices with their start and end apart: 1 -> 0, of which waited for: 1 -> 0; matrix products, arithmetic and copies ran while one was open for 0% -> 0% of each run, Pallas kernels for 0% -> 0%
where the time goes in v3:
time: 246 us
  Pallas kernels  244 us (99%)
    pallas_call x1, Pallas kernels, reduce_grams(): pl.pallas_call(reduce_kernel, out_shape=jax.ShapeDtypeStruct((3, PACKED,...  110 us
    pallas_call x1, Pallas kernels, gather(): pl.pallas_call(gather_kernel, out_shape=jax.ShapeDtypeStruct((SIDE, SIDE,...  75.1 us
    pallas_call x1, Pallas kernels, solve(): pl.pallas_call(solve_kernel, out_shape=jax.ShapeDtypeStruct((d, e), jnp.b...  37.4 us
    pallas_call x1, Pallas kernels, beams(): pl.pallas_call(apply_kernel, grid=(bins // step,), out_shape=jax.ShapeDty...  21.4 us

profile of v3, /device:TPU:1, one launch (start us, length us, event | category | flops | bytes accessed | tf_op | source)
XLA Modules:
  0.0 245.7 jit_solution(4191259840887524270)
XLA Ops:
  0.7 0.8 convert_reduce_fusion
  1.4 0.6 broadcast_in_dim.2.chosen_ref
  2.0 109.7 %reduce_grams.1.gram_ref = f32[3,200,128]{2,1,0:T(8,128)} custom-call(bf16[4,4,4,2,128,384]{5,4,3,2,1,0:T(8,128)(2,1)} %bitcast.7, f32[8,128]{1,0:T(8,128)} %broadcast_in_dim.2.chosen_ref), custom_call_target="tpu_custom_call" | custom-call | tf_op jit(solution)/shard_map/reduce_grams/pallas_call | solution.py:456
  111.8 37.4 %solve.1.own_ref = bf16[384,256]{1,0:T(8,128)(2,1)} custom-call(s32[1]{0:T(128)} %copy.5.count_ref, f32[3,200,128]{2,1,0:T(8,128)} %reduce_grams.1.gram_ref, bf16[384,256]{1,0:T(8,128)(2,1)} %bitcast.8), custom_call_target="tpu_custom_call" | custom-call | tf_op jit(solution)/shard_map/solve/pallas_call | solution.py:85
  149.2 75.1 %gather.1 = bf16[4,4,4,2,384,256]{5,4,3,2,1,0:T(8,128)(2,1)} custom-call(bf16[384,256]{1,0:T(8,128)(2,1)} %solve.1.own_ref), custom_call_target="tpu_custom_call" | custom-call | tf_op jit(solution)/shard_map/gather/pallas_call | solution.py:192
  224.3 21.4 %beams.1 = bf16[128,128,256]{2,1,0:T(8,128)(2,1)} custom-call(bf16[128,128,384]{2,1,0:T(8,128)(2,1)} %snap_ref.1, bf16[128,384,256]{2,1,0:T(8,128)(2,1)} %bitcast.6), custom_call_target="tpu_custom_call" | custom-call | tf_op jit(solution)/shard_map/beams/pallas_call | solution.py:211
  (2 shorter events, 0.0 us)

commit v4 on v2

--- a/solution.py
+++ b/solution.py
@@ -6,8 +6,6 @@
 from jax.sharding import PartitionSpec as P
 
 BLOCK = 128
-
-
 LOADING = 0.1
 
 
@@ -20,7 +18,7 @@
 
 
 HI = lax.Precision.HIGHEST
-T = 128
+T = BLOCK
 def mm(a, b, ca, cb):
     return lax.dot_general(a, b, (((ca,), (cb,)), ((), ())), precision=HI, preferred_element_type=jnp.float32)
 
@@ -50,24 +48,313 @@
     unit = jnp.where(i > j, full, jnp.where(i == j, 1.0, 0.0))
     return unit * lax.rsqrt(pivots)
 
-def solve_kernel(count_ref, gram_ref, steer_ref, out_ref, cov, rhs, inv):
-    n = gram_ref.shape[0] // T
+
+MESH = pl.DeviceIdType.MESH
+SIDE = 4
+ORDERS = (("x", "y", "z"), ("y", "z", "x"), ("z", "x", "y"))
+
+def place():
+    r, d = lax.axis_index("range"), lax.axis_index("doppler")
+    return {"z": r // SIDE, "y": r % SIDE, "x": d // 2, "c": d % 2}
+
+def device(at):
+    return (at["z"] * SIDE + at["y"], at["x"] * 2 + at["c"])
+
+def moved(at, axis, step):
+    return {**at, axis: (at[axis] + step) % SIDE}
+
+def twin(at):
+    return {**at, "c": 1 - at["c"]}
+
+def greet(at):
+    barrier = pltpu.get_barrier_semaphore()
+    friends = [moved(at, a, s) for a in "xyz" for s in (1, SIDE - 1)] + [twin(at)]
+    for friend in friends:
+        pl.semaphore_signal(barrier, inc=1, device_id=device(friend), device_id_type=MESH)
+    pl.semaphore_wait(barrier, len(friends))
+
+HALF = 64
+PACKED = 200
+CUT = 104
+TOP, LOW, ALL = (0, CUT), (CUT, PACKED - CUT), (0, PACKED)
+REDUCE = (("z", "y", "x"), ("x", "z", "y"), ("y", "x", "z"))
+
+def cross(a, b):
+    return lax.dot_general(a, b, (((0,), (0,)), ((), ())), preferred_element_type=jnp.float32)
+
+def packed_part(part, snaps):
+    first, second, third = snaps[:, :T], snaps[:, T:2 * T], snaps[:, 2 * T:]
+    i = lax.broadcasted_iota(jnp.int32, (HALF, T), 0)
+    j = lax.broadcasted_iota(jnp.int32, (HALF, T), 1)
+    if part == 2:
+        both = cross(third, jnp.concatenate([first, third], axis=1))
+        tile, square = both[:, :T], both[:, T:]
+        turned = pltpu.roll(square[:HALF], HALF, axis=1)
+        fold = jnp.where(j - HALF > i, turned, square[HALF:])
+        ridge = jnp.where(j - HALF == i, turned, 0.0)
+    else:
+        lo = part * HALF
+        lower = cross(first, first)[lo:lo + HALF]
+        if part == 0:
+            both = cross(second, snaps[:, :2 * T])
+            tile, upper = both[:, :T], both[lo:lo + HALF, T:]
+        else:
+            both = cross(second, snaps[:, T:])
+            tile, upper = both[:, T:], both[lo:lo + HALF, :T]
+        fold = jnp.where(j <= i + lo, lower, upper)
+        ridge = jnp.where(j == i + lo, upper, 0.0)
+    return tile, fold, jnp.broadcast_to(jnp.sum(ridge, axis=0, keepdims=True), (8, T))
+
+def unpack(packed, roll):
+    i = lax.broadcasted_iota(jnp.int32, (T, T), 0)
+    j = lax.broadcasted_iota(jnp.int32, (T, T), 1)
+    fold = jnp.concatenate([packed[0, T:T + HALF], packed[1, T:T + HALF]], axis=0)
+    ridge = packed[0, PACKED - 8:PACKED - 7] + packed[1, PACKED - 8:PACKED - 7]
+    t00 = jnp.where(j <= i, fold, fold.T)
+    t11 = jnp.where(j > i, fold, jnp.where(i == j, ridge, fold.T))
+    low = packed[2, T:T + HALF]
+    mixed = jnp.concatenate([roll(low, HALF, 1), low], axis=0)
+    ridge = roll(packed[2, PACKED - 8:], HALF, 1)[:1]
+    keep = ((i < HALF) & (j < HALF) & (j > i)) | ((i >= HALF) & (j <= i))
+    t22 = jnp.where((i == j) & (i < HALF), ridge, jnp.where(keep, mixed, mixed.T))
+    return t00, packed[0, :T], t11, packed[2, :T], packed[1, :T].T, t22
+
+def reduce_phase(at, snap_ref, chosen_ref, out_ref, go, own, other, marks, grams, far1, down1, up1, far2, down2, up2, far3, down3, up3,
+                  own_sem, twin_send, twin_recv, mark_send, mark_recv, send1, recv1, send2, recv2):
+    twin_at = twin(at)
+    me = ((at["z"] * SIDE + at["y"]) * SIDE + at["x"]) * 2
+    far = (far1, far2, far3)
+    down_in = (down1, down2, down3)
+    up_in = (up1, up2, up3)
+
+    def turn(axis, step):
+        return (at[axis] + step) % SIDE
+
+    def own_copy(z):
+        return pltpu.make_async_copy(snap_ref.at[z, :, :, at["c"]], own.at[z], own_sem.at[z])
+    def twin_copy(z):
+        return pltpu.make_async_remote_copy(
+            src_ref=snap_ref.at[z, :, :, twin_at["c"]], dst_ref=other.at[z], send_sem=twin_send.at[z], recv_sem=twin_recv.at[z],
+            device_id=device(twin_at), device_id_type=MESH)
+    order = [turn("z", s) for s in (2, 1, 3, 0)]
+
+    def mark_copy(stage, kind):
+        axis = "xyz"[stage]
+        where = moved(at, axis, SIDE - 1) if kind == 2 else at
+        ref = marks.at[(where["z"], where["y"], where["x"])[:SIDE - 1 - stage]]
+        target = moved(at, axis, SIDE - 1 if kind == 1 else 1)
+        return pltpu.make_async_remote_copy(
+            src_ref=ref, dst_ref=ref, send_sem=mark_send.at[stage, kind], recv_sem=mark_recv.at[stage, kind],
+            device_id=device(target), device_id_type=MESH)
+    for z in order:
+        twin_copy(z).start()
+        own_copy(z).start()
+    marks[at["z"], at["y"], at["x"]] = chosen_ref[...]
+    for stage in range(3):
+        mark_copy(stage, 0).start()
+        mark_copy(stage, 1).start()
+        mark_copy(stage, 0).wait_recv()
+        mark_copy(stage, 2).start()
+        mark_copy(stage, 1).wait_recv()
+        mark_copy(stage, 2).wait_recv()
+    for stage in range(3):
+        for kind in range(3):
+            mark_copy(stage, kind).wait_send()
+
+    lane = lax.broadcasted_iota(jnp.int32, (1, T), 1)
+    def ready(z):
+        own_copy(z).wait()
+        twin_copy(z).wait_recv()
+        def mask(n, carry):
+            y, x = n // SIDE, n % SIDE
+            row = marks[z, y, x][:1]
+            for ref, block in ((own, me + at["c"]), (other, me + twin_at["c"])):
+                keep = jnp.sum(jnp.where(lane == block, row, 0.0), axis=1, keepdims=True)
+                ref[z, y, x] = (ref[z, y, x].astype(jnp.float32) * keep).astype(jnp.bfloat16)
+            return carry
+        lax.fori_loop(0, SIDE * SIDE, mask, 0, unroll=4)
+
+    def compute(part, i3, i2):
+        names = REDUCE[part]
+        def one(i1, carry):
+            where = dict(zip(names, (i3, i2, i1)))
+            spot = (where["z"], where["y"], where["x"])
+            snaps = jnp.concatenate([own[spot], other[spot]], axis=0)
+            tile, fold, ridge = packed_part(part, snaps)
+            grams[part, i3, i2, i1, 0:T] = tile
+            grams[part, i3, i2, i1, T:T + HALF] = fold
+            grams[part, i3, i2, i1, T + HALF:PACKED] = ridge
+            return carry
+        lax.fori_loop(0, SIDE, one, 0, unroll=True)
+
+    KIND = (
+        (2, TOP, "far", 1), (2, LOW, "far", SIDE - 1), (1, LOW, "near", 1),
+        (SIDE - 1, TOP, "near", SIDE - 1), (1, TOP, "near", 1), (SIDE - 1, LOW, "near", SIDE - 1),
+    )
+    def hop(part, stage, kind, chunk=None):
+        step, (lo, count), slot, way = KIND[kind]
+        names = REDUCE[part]
+        prefix = tuple(at[a] for a in names[:stage])
+        tail = () if chunk is None else (chunk,)
+        rows = (slice(None),) * (2 - stage - len(tail)) + (pl.ds(lo, count), slice(None))
+        src = grams.at[(part,) + prefix + (turn(names[stage], step),) + tail + rows]
+        box = far[stage] if slot == "far" else (down_in[stage] if way == 1 else up_in[stage])
+        dst = box.at[(part,) + tail + rows]
+        if chunk is None:
+            ss, rs = send2.at[part, stage - 1, kind], recv2.at[part, stage - 1, kind]
+        else:
+            ss, rs = send1.at[part, kind, chunk], recv1.at[part, kind, chunk]
+        return pltpu.make_async_remote_copy(
+            src_ref=src, dst_ref=dst, send_sem=ss, recv_sem=rs,
+            device_id=device(moved(at, names[stage], way)), device_id_type=MESH)
+
+    def add_far(part, stage, kind, chunk=None):
+        names = REDUCE[part]
+        prefix = tuple(at[a] for a in names[:stage])
+        tail = () if chunk is None else (chunk,)
+        step, (lo, count) = (1, TOP) if kind == 0 else (SIDE - 1, LOW)
+        whole = (slice(None),) * (2 - stage - len(tail)) + (slice(lo, lo + count), slice(None))
+        spot = (part,) + prefix + (turn(names[stage], step),) + tail + whole
+        grams[spot] = grams[spot] + far[stage][(part,) + tail + whole]
+
+    def add_near(part, stage, chunk=None):
+        names = REDUCE[part]
+        tail = () if chunk is None else (chunk,)
+        spot = (part,) + tuple(at[a] for a in names[:stage + 1]) + tail
+        got = (part,) + tail
+        grams[spot] = grams[spot] + down_in[stage][got] + up_in[stage][got]
+
+    def second(part, q):
+        return (at[REDUCE[part][1]] + 6 - q) % SIDE
+
+    def loop(body):
+        def run(q, carry):
+            body(q)
+            return carry
+        lax.fori_loop(0, SIDE, run, 0)
+
+    leads = at["c"] == 0
+
+    def compute_first(part, i3, i2):
+        pl.when(leads)(lambda: compute(part, i3, i2))
+
+    def far_out(part):
+        def body(q):
+            compute_first(part, turn(REDUCE[part][0], 2), second(part, q))
+            hop(part, 0, 0, second(part, q)).start()
+            hop(part, 0, 1, second(part, q)).start()
+        loop(body)
+
+    ready(order[0])
+    pl.when(leads)(lambda: far_out(0))
+    for z in order[1:]:
+        ready(z)
+
+    @pl.when(jnp.logical_not(leads))
+    def _():
+        for part in range(3):
+            def every(n, carry):
+                compute(part, n // SIDE, n % SIDE)
+                return carry
+            lax.fori_loop(0, SIDE * SIDE, every, 0)
+        pl.semaphore_wait(go, 1)
+        far_out(0)
+
+    far_out(1)
+    far_out(2)
+
+    def near_out(q):
+        for part in range(3):
+            for step, kind in ((1, 2), (SIDE - 1, 3)):
+                compute_first(part, turn(REDUCE[part][0], step), second(part, q))
+                hop(part, 0, kind, second(part, q)).start()
+    loop(near_out)
+
+    def relay(q):
+        for part in range(3):
+            compute_first(part, at[REDUCE[part][0]], second(part, q))
+        for part in range(3):
+            chunk = second(part, q)
+            for kind in (0, 1):
+                hop(part, 0, kind, chunk).wait_recv()
+                add_far(part, 0, kind, chunk)
+                hop(part, 0, kind + 4, chunk).start()
+    loop(relay)
+
+    for q in range(SIDE):
+        for part in range(3):
+            chunk = second(part, q)
+            for kind in (2, 3, 4, 5):
+                hop(part, 0, kind, chunk).wait_recv()
+            add_near(part, 0, chunk)
+            for kind in ((0, 1), (2,), (), (3,))[q]:
+                hop(part, 1, kind).start()
+    @pl.when(leads)
+    def _():
+        pl.semaphore_signal(go, inc=1, device_id=device(twin_at), device_id_type=MESH)
+
+    for stage in (1, 2):
+        for part in range(3):
+            for kind in (0, 1):
+                hop(part, stage, kind).wait_recv()
+                add_far(part, stage, kind)
+                hop(part, stage, kind + 4).start()
+        for part in range(3):
+            for kind in (2, 3, 4, 5):
+                hop(part, stage, kind).wait_recv()
+            add_near(part, stage)
+            if stage == 1:
+                for kind in range(4):
+                    hop(part, 2, kind).start()
+    for part in range(3):
+        out_ref[part] = grams[(part,) + tuple(at[a] for a in REDUCE[part])]
+
+    for z in order:
+        twin_copy(z).wait_send()
+    def drain(q):
+        for part in range(3):
+            for kind in range(6):
+                hop(part, 0, kind, q).wait_send()
+    loop(drain)
+    for part in range(3):
+        for stage in (1, 2):
+            for kind in range(6):
+                hop(part, stage, kind).wait_send()
+
+
+def solve_phase(count_ref, packed, steer_ref, out_ref, diag, cov, rhs, inv):
+    n = cov.shape[0] // T
     scale = (BLOCK * count_ref[0]).astype(jnp.float32)
-    i = lax.broadcasted_iota(jnp.int32, cov.shape, 0)
-    j = lax.broadcasted_iota(jnp.int32, cov.shape, 1)
-    cov[...] = gram_ref[...] / scale + jnp.where(i == j, LOADING, 0.0)
+    i = lax.broadcasted_iota(jnp.int32, (T, T), 0)
+    j = lax.broadcasted_iota(jnp.int32, (T, T), 1)
+    tiles = unpack(packed, pltpu.roll)
+    for (r, c), tile in zip(((0, 0), (1, 0), (1, 1), (2, 0), (2, 1), (2, 2)), tiles):
+        tile = tile / scale
+        if r == c:
+            diag[r] = tile + jnp.where(i == j, LOADING, 0.0)
+        else:
+            cov[r * T:(r + 1) * T, c * T:(c + 1) * T] = tile
     rhs[...] = steer_ref[...].astype(jnp.float32)
-    for b in range(n):
-        lo, hi = b * T, (b + 1) * T
-        inv[b] = factor_inverse(cov[lo:hi, lo:hi])
-        li = inv[b]
-        y = mm(li, rhs[lo:hi, :], 1, 0)
-        rhs[lo:hi, :] = y
-        if b + 1 < n:
-            panel = mm(cov[hi:, lo:hi], li, 1, 1)
-            cov[hi:, lo:hi] = panel
-            cov[hi:, hi:] = cov[hi:, hi:] - mm(panel, panel, 1, 1)
-            rhs[hi:, :] = rhs[hi:, :] - mm(panel, y, 1, 0)
+
+    def forward(b, carry):
+        inv[b] = factor_inverse(diag[b])
+        for which in range(n):
+            def update(b=which):
+                lo, hi = b * T, (b + 1) * T
+                li = inv[b]
+                y = mm(li, rhs[lo:hi, :], 1, 0)
+                rhs[lo:hi, :] = y
+                if b + 1 < n:
+                    panel = mm(cov[hi:, lo:hi], li, 1, 1)
+                    cov[hi:, lo:hi] = panel
+                    diag[b + 1] = diag[b + 1] - mm(panel[:T], panel[:T], 1, 1)
+                    rhs[hi:, :] = rhs[hi:, :] - mm(panel, y, 1, 0)
+                if b + 2 < n:
+                    diag[b + 2] = diag[b + 2] - mm(panel[T:], panel[T:], 1, 1)
+                    cov[hi + T:, hi:hi + T] = cov[hi + T:, hi:hi + T] - mm(panel[T:], panel[:T], 1, 1)
+            pl.when(b == which)(update)
+        return carry
+    lax.fori_loop(0, n, forward, 0)
     for b in reversed(range(n)):
         lo, hi = b * T, (b + 1) * T
         y = rhs[lo:hi, :]
@@ -78,47 +365,10 @@
     response = jnp.sum(steer_ref[...].astype(jnp.float32) * solved, axis=0, keepdims=True)
     out_ref[...] = (solved / response).astype(out_ref.dtype)
 
-def solve(count, gram, steer):
-    d, e = steer.shape
-    return pl.pallas_call(
-        solve_kernel,
-        out_shape=jax.ShapeDtypeStruct((d, e), jnp.bfloat16),
-        in_specs=[pl.BlockSpec(memory_space=pltpu.SMEM), pl.BlockSpec(memory_space=pltpu.VMEM), pl.BlockSpec(memory_space=pltpu.VMEM)],
-        out_specs=pl.BlockSpec(memory_space=pltpu.VMEM),
-        scratch_shapes=[pltpu.VMEM((d, d), jnp.float32), pltpu.VMEM((d, e), jnp.float32), pltpu.VMEM((d // T, T, T), jnp.float32)],
-        name="solve",
-    )(count, gram, steer)
-
-
-MESH = pl.DeviceIdType.MESH
-SIDE = 4
-ORDERS = (("x", "y", "z"), ("y", "z", "x"), ("z", "x", "y"))
-
-def place():
-    r, d = lax.axis_index("range"), lax.axis_index("doppler")
-    return {"z": r // SIDE, "y": r % SIDE, "x": d // 2, "c": d % 2}
-
-def device(at):
-    return (at["z"] * SIDE + at["y"], at["x"] * 2 + at["c"])
-
-def moved(at, axis, step):
-    return {**at, axis: (at[axis] + step) % SIDE}
-
-def twin(at):
-    return {**at, "c": 1 - at["c"]}
-
-def greet(at):
-    barrier = pltpu.get_barrier_semaphore()
-    friends = [moved(at, a, s) for a in "xyz" for s in (1, SIDE - 1)] + [twin(at)]
-    for friend in friends:
-        pl.semaphore_signal(barrier, inc=1, device_id=device(friend), device_id_type=MESH)
-    pl.semaphore_wait(barrier, len(friends))
-
-def gather_kernel(own_ref, all_ref, local_sem, send_sem, recv_sem, twin_send, twin_recv):
-    at = place()
+
+def gather_phase(at, own_ref, all_ref, local_sem, send_sem, recv_sem, twin_send, twin_recv):
     rows = own_ref.shape[0] // 3
     half = rows // 2
-    greet(at)
 
     def window(part, gathered, where, halves):
         lo, count = (part * rows, rows) if halves is None else (part * rows + halves * half, half)
@@ -185,25 +435,48 @@
             src_ref=ref, dst_ref=ref, send_sem=twin_send.at[part, stage, kind], recv_sem=twin_recv.at[part, stage, kind],
             device_id=device(twin(at)), device_id_type=MESH).wait_recv()
 
-def gather(own):
-    rows, columns = own.shape
+
+def adapt_kernel(count_ref, snap_ref, chosen_ref, steer_ref, all_ref, packed, weights, diag, cov, rhs, inv, go, *scratch):
+    at = place()
+    greet(at)
+    reduce_phase(at, snap_ref, chosen_ref, packed, go, *scratch[:-5])
+    solve_phase(count_ref, packed, steer_ref, weights, diag, cov, rhs, inv)
+    gather_phase(at, weights, all_ref, *scratch[-5:])
+
+
+def adapt(snapshots, chosen, train_count, steering):
+    bins, gates, channels = snapshots.shape
+    looks = steering.shape[1]
+    split = snapshots.reshape(SIDE, SIDE, SIDE, 2, gates, channels)
+    f32, bf16, sem = jnp.float32, jnp.bfloat16, pltpu.SemaphoreType.DMA
+    boxes = [pltpu.VMEM((3,) + (SIDE,) * n + (PACKED, T), f32) for n in (2, 2, 2, 1, 1, 1, 0, 0, 0)]
+    vmem = pl.BlockSpec(memory_space=pltpu.VMEM)
     whole = pl.pallas_call(
-        gather_kernel,
-        out_shape=jax.ShapeDtypeStruct((SIDE, SIDE, SIDE, 2, rows, columns), own.dtype),
-        in_specs=[pl.BlockSpec(memory_space=pltpu.VMEM)],
+        adapt_kernel,
+        out_shape=jax.ShapeDtypeStruct((SIDE, SIDE, SIDE, 2, channels, looks), bf16),
+        in_specs=[pl.BlockSpec(memory_space=pltpu.SMEM), pl.BlockSpec(memory_space=pl.ANY), vmem, vmem],
         out_specs=pl.BlockSpec(memory_space=pl.ANY),
-        scratch_shapes=[pltpu.SemaphoreType.DMA, pltpu.SemaphoreType.DMA((3, 3, 6)), pltpu.SemaphoreType.DMA((3, 3, 6)),
-                        pltpu.SemaphoreType.DMA((3, 4, 6)), pltpu.SemaphoreType.DMA((3, 4, 6))],
-        compiler_params=pltpu.CompilerParams(collective_id=1, has_side_effects=True),
-        name="gather",
-    )(own)
-    return whole.reshape(SIDE * SIDE * SIDE * 2, rows, columns)
+        scratch_shapes=[
+            pltpu.VMEM((3, PACKED, T), f32), pltpu.VMEM((channels, looks), bf16), pltpu.VMEM((channels // T, T, T), f32),
+            pltpu.VMEM((channels, channels), f32), pltpu.VMEM((channels, looks), f32), pltpu.VMEM((channels // T, T, T), f32),
+            pltpu.SemaphoreType.REGULAR,
+            pltpu.VMEM((SIDE, SIDE, SIDE, gates, channels), bf16), pltpu.VMEM((SIDE, SIDE, SIDE, gates, channels), bf16),
+            pltpu.VMEM((SIDE, SIDE, SIDE, 8, T), f32), pltpu.VMEM((3, SIDE, SIDE, SIDE, PACKED, T), f32), *boxes,
+            sem((SIDE,)), sem((SIDE,)), sem((SIDE,)), sem((3, 3)), sem((3, 3)),
+            sem((3, 6, SIDE)), sem((3, 6, SIDE)), sem((3, 2, 6)), sem((3, 2, 6)),
+            sem, sem((3, 3, 6)), sem((3, 3, 6)), sem((3, 4, 6)), sem((3, 4, 6)),
+        ],
+        compiler_params=pltpu.CompilerParams(collective_id=1, has_side_effects=True, vmem_limit_bytes=67000000),
+        name="adapt",
+    )(train_count, split, chosen, steering)
+    return whole.reshape(bins, channels, looks)
+
 
 def apply_kernel(snap_ref, weight_ref, out_ref):
     for b in range(snap_ref.shape[0]):
         out_ref[b] = jnp.dot(snap_ref[b], weight_ref[b], preferred_element_type=jnp.float32).astype(out_ref.dtype)
 
-def beams(snapshots, weights, step=8):
+def beams(snapshots, weights, step=16):
     bins, gates, channels = snapshots.shape
     looks = weights.shape[2]
     return pl.pallas_call(
@@ -216,27 +489,10 @@
     )(snapshots, weights)
 
 
-def adapt(own_snaps, train_list, train_count, steering):
-    own_bins, gate_total, channels = own_snaps.shape
-    block_total = train_list.shape[1]
-    chosen = selection(train_list, train_count)
-    blocks = own_snaps.reshape(own_bins, block_total, gate_total // block_total, channels)
-    masked = blocks * chosen.astype(own_snaps.dtype)[:, :, None, None]
-    gram_sum = jnp.einsum("bnrd,bnre->bde", masked, blocks, preferred_element_type=jnp.float32)
-    return solve(train_count, gram_sum[0], steering[0])[None]
-
-
 def body(snapshots, steering, train_list, train_count):
-    bin_total, gate_rows, channels = snapshots.shape
-    own_bins = steering.shape[0]
-    devices = bin_total // own_bins
-    outgoing = snapshots.reshape(devices, own_bins, gate_rows, channels)
-    arrived = lax.all_to_all(
-        outgoing, ("range", "doppler"), split_axis=0, concat_axis=0, tiled=True
-    )
-    own_snaps = jnp.moveaxis(arrived, 1, 0).reshape(own_bins, devices * gate_rows, channels)
-    weights = adapt(own_snaps, train_list, train_count, steering)
-    return beams(snapshots, gather(weights[0]))
+    chosen = selection(train_list, train_count).astype(jnp.float32)
+    weights = adapt(snapshots, jnp.broadcast_to(chosen, (8, BLOCK)), train_count, steering[0])
+    return beams(snapshots, weights)
 
 
 def solution(mesh):

time: 324 us -> 216 us (0.67)
  waiting for transfers between devices: 151 us -> 0 us
  Pallas kernels: 144 us -> 214 us
  matrix products: 15.9 us -> 0 us
  starting transfers between devices: 11.9 us -> 0 us
    all_to_all x1 -> x0, waiting for transfers between devices: 151 us -> none  [body(): lax.all_to_all(outgoing, ('range', 'doppler'), split_axis=0, concat_axis=...]
    pallas_call x2 -> x1, Pallas kernels: 123 us -> 196 us  [adapt(): pl.pallas_call(adapt_kernel, out_shape=jax.ShapeDtypeStruct((SIDE, SIDE,...]
    dot_general x1 -> x0, matrix products: 15.9 us -> none  [adapt(): jnp.einsum('bnrd,bnre->bde', masked, blocks, preferred_element_type=jnp.f...]
    all_to_all x1 -> x0, starting transfers between devices: 11.9 us -> none  [body(): lax.all_to_all(outgoing, ('range', 'doppler'), split_axis=0, concat_axis=...]
    pallas_call x1, Pallas kernels: 21.4 us -> 17.4 us  [beams(): pl.pallas_call(apply_kernel, grid=(bins // step,), out_shape=jax.ShapeDty...]
  transfers between devices with their start and end apart: 1 -> 0, of which waited for: 1 -> 0; matrix products, arithmetic and copies ran while one was open for 0% -> 0% of each run, Pallas kernels for 0% -> 0%
where the time goes in v4:
time: 216 us
  Pallas kernels  214 us (99%)
    pallas_call x1, Pallas kernels, adapt(): pl.pallas_call(adapt_kernel, out_shape=jax.ShapeDtypeStruct((SIDE, SIDE,...  196 us
    pallas_call x1, Pallas kernels, beams(): pl.pallas_call(apply_kernel, grid=(bins // step,), out_shape=jax.ShapeDty...  17.4 us

profile of v4, /device:TPU:1, one launch (start us, length us, event | category | flops | bytes accessed | tf_op | source)
XLA Modules:
  0.0 215.9 jit_solution(10547491517732923047)
XLA Ops:
  0.7 0.8 convert_reduce_fusion
  1.4 0.6 broadcast_in_dim.2.chosen_ref
  2.0 196.5 %adapt.1 = bf16[4,4,4,2,384,256]{5,4,3,2,1,0:T(8,128)(2,1)} custom-call(s32[1]{0:T(128)} %copy.5.count_ref, bf16[4,4,4,2,128,384]{5,4,3,2,1,0:T(8,128)(2,1)} %bitcast.7, f32[8,128]{1,0:T(8,128)} %broadcast_in_dim.2.chosen_ref, bf16[384,256]{1,0:T(8,128)(2,1)} %bitcast.8), custom_call_target="tpu_custom_call" | custom-call | tf_op jit(solution)/shard_map/adapt/pallas_call | solution.py:454
  198.5 17.4 %beams.1 = bf16[128,128,256]{2,1,0:T(8,128)(2,1)} custom-call(bf16[128,128,384]{2,1,0:T(8,128)(2,1)} %snap_ref.1, bf16[128,384,256]{2,1,0:T(8,128)(2,1)} %bitcast.6), custom_call_target="tpu_custom_call" | custom-call | tf_op jit(solution)/shard_map/beams/pallas_call | solution.py:482
  (2 shorter events, 0.0 us)

commit v5 on v4

--- a/solution.py
+++ b/solution.py
@@ -25,32 +25,55 @@
 def factor_inverse(block):
     lane = lax.broadcasted_iota(jnp.int32, (8, T), 1)
     sub = lax.broadcasted_iota(jnp.int32, (8, T), 0)
-    rows = [block[8 * g:8 * g + 8, :] for g in range(T // 8)]
-    for k in range(T):
+    groups = T // 8
+    rows = [block[8 * g:8 * g + 8, :] for g in range(groups)]
+
+    def spread(g, k):
+        return jnp.broadcast_to(rows[g][:, k:k + 1], (8, T))
+    left = [spread(g, 0) for g in range(groups)]
+    right = [spread(g, 1) for g in range(groups)]
+    for k in range(0, T, 2):
         own, off = k // 8, k % 8
-        row = rows[own][off:off + 1, :]
-        inv = 1.0 / row[:, k:k + 1]
-        scaled = jnp.where(lane[:1] == k, 1.0, row) * inv
-        for g in range(own, T // 8):
-            col = rows[g][:, k:k + 1]
+        if k:
+            left = [None if f is None else x - f * tips[0] - h * tips[1] for x, f, h in zip(next_left, first, second)]
+            right = [None if f is None else x - f * tips[2] - h * tips[3] for x, f, h in zip(next_right, first, second)]
+        a, b, d = left[own][off:off + 1], left[own][off + 1:off + 2], right[own][off + 1:off + 2]
+        inv = 1.0 / (a * d - b * b)
+        aa, ab, bb = d * inv, b * inv, a * inv
+        top, low = rows[own][off:off + 1], rows[own][off + 1:off + 2]
+        follow = (k + 2) // 8
+        if k + 2 < T:
+            next_left = [spread(g, k + 2) if g >= follow else None for g in range(groups)]
+            next_right = [spread(g, k + 3) if g >= follow else None for g in range(groups)]
+            tips = [jnp.broadcast_to(r[:, n:n + 1], (1, T)) for n in (k + 2, k + 3) for r in (top, low)]
+        pair = (lane == k) | (lane == k + 1)
+        top = jnp.where(pair[:1], jnp.where(lane[:1] == k, 1.0, 0.0), top)
+        low = jnp.where(pair[:1], jnp.where(lane[:1] == k, 0.0, 1.0), low)
+        first, second = [None] * groups, [None] * groups
+        for g in range(follow, groups):
+            f = left[g] * aa - right[g] * ab
+            h = right[g] * bb - left[g] * ab
+            base = jnp.where(pair, 0.0, rows[g])
             if g == own:
-                if off == 7:
-                    continue
-                col = jnp.where(sub[:, :1] > off, col, 0.0)
-                base = jnp.where((lane == k) & (sub > off), 0.0, rows[g])
-            else:
-                base = jnp.where(lane == k, 0.0, rows[g])
-            rows[g] = base - col * scaled
+                f = jnp.where(sub > off + 1, f, 0.0)
+                h = jnp.where(sub > off + 1, h, 0.0)
+                base = jnp.where(sub > off + 1, base, rows[g])
+            first[g], second[g] = f, h
+            rows[g] = base - f * top - h * low
     full = jnp.concatenate(rows, axis=0)
     i = lax.broadcasted_iota(jnp.int32, (T, T), 0)
     j = lax.broadcasted_iota(jnp.int32, (T, T), 1)
-    pivots = jnp.sum(jnp.where(i == j, full, 0.0), axis=1, keepdims=True)
-    unit = jnp.where(i > j, full, jnp.where(i == j, 1.0, 0.0))
-    return unit * lax.rsqrt(pivots)
+    odd = i % 2 == 1
+    pivots = jnp.broadcast_to(jnp.sum(jnp.where(i == j, full, 0.0), axis=1, keepdims=True), (T, T))
+    below = jnp.sum(jnp.where(odd & (j == i - 1), full, 0.0), axis=1, keepdims=True)
+    unit = jnp.where(j < i - i % 2, full, jnp.where(i == j, 1.0, 0.0))
+    ratio = jnp.where(odd, below / pltpu.roll(pivots, 1, axis=0), 0.0)
+    return (unit - ratio * pltpu.roll(unit, 1, axis=0)) * lax.rsqrt(pivots - below * ratio)
 
 
 MESH = pl.DeviceIdType.MESH
 SIDE = 4
+SLICES = 1
 ORDERS = (("x", "y", "z"), ("y", "z", "x"), ("z", "x", "y"))
 
 def place():
@@ -68,7 +91,7 @@
 
 def greet(at):
     barrier = pltpu.get_barrier_semaphore()
-    friends = [moved(at, a, s) for a in "xyz" for s in (1, SIDE - 1)] + [twin(at)]
+    friends = [moved(at, a, s) for a in "xyz" for s in range(1, SIDE)] + [twin(at)]
     for friend in friends:
         pl.semaphore_signal(barrier, inc=1, device_id=device(friend), device_id_type=MESH)
     pl.semaphore_wait(barrier, len(friends))
@@ -139,24 +162,20 @@
     order = [turn("z", s) for s in (2, 1, 3, 0)]
 
     def mark_copy(stage, kind):
-        axis = "xyz"[stage]
-        where = moved(at, axis, SIDE - 1) if kind == 2 else at
-        ref = marks.at[(where["z"], where["y"], where["x"])[:SIDE - 1 - stage]]
-        target = moved(at, axis, SIDE - 1 if kind == 1 else 1)
+        ref = marks.at[(at["z"], at["y"], at["x"])[:SIDE - 1 - stage]]
+        target = moved(at, "xyz"[stage], kind + 1)
         return pltpu.make_async_remote_copy(
             src_ref=ref, dst_ref=ref, send_sem=mark_send.at[stage, kind], recv_sem=mark_recv.at[stage, kind],
             device_id=device(target), device_id_type=MESH)
     for z in order:
         twin_copy(z).start()
         own_copy(z).start()
-    marks[at["z"], at["y"], at["x"]] = chosen_ref[...]
+    marks[at["z"], at["y"], at["x"]] = jnp.broadcast_to(chosen_ref[...], (8, T))
     for stage in range(3):
-        mark_copy(stage, 0).start()
-        mark_copy(stage, 1).start()
-        mark_copy(stage, 0).wait_recv()
-        mark_copy(stage, 2).start()
-        mark_copy(stage, 1).wait_recv()
-        mark_copy(stage, 2).wait_recv()
+        for kind in range(3):
+            mark_copy(stage, kind).start()
+        for kind in range(3):
+            mark_copy(stage, kind).wait_recv()
     for stage in range(3):
         for kind in range(3):
             mark_copy(stage, kind).wait_send()
@@ -170,7 +189,8 @@
             row = marks[z, y, x][:1]
             for ref, block in ((own, me + at["c"]), (other, me + twin_at["c"])):
                 keep = jnp.sum(jnp.where(lane == block, row, 0.0), axis=1, keepdims=True)
-                ref[z, y, x] = (ref[z, y, x].astype(jnp.float32) * keep).astype(jnp.bfloat16)
+                keep = jnp.broadcast_to(keep, (1, ref.shape[-1])).astype(jnp.bfloat16)
+                ref[z, y, x] = ref[z, y, x] * keep
             return carry
         lax.fori_loop(0, SIDE * SIDE, mask, 0, unroll=4)
 
@@ -367,7 +387,7 @@
 
 
 def gather_phase(at, own_ref, all_ref, local_sem, send_sem, recv_sem, twin_send, twin_recv):
-    rows = own_ref.shape[0] // 3
+    rows = own_ref.shape[0] // (3 * SLICES)
     half = rows // 2
 
     def window(part, gathered, where, halves):
@@ -375,65 +395,74 @@
         pick = tuple(slice(None) if a in gathered else where[a] for a in "zyx")
         return all_ref.at[pick + (where["c"], pl.ds(lo, count), slice(None))]
 
-    pending = []
+    def copy(part, stage, kind, gathered, where, halves, target, send, recv, src=None):
+        ref = window(part, gathered, where, halves)
+        return pltpu.make_async_remote_copy(
+            src_ref=ref if src is None else src, dst_ref=ref, send_sem=send.at[part, stage, kind], recv_sem=recv.at[part, stage, kind],
+            device_id=device(target), device_id_type=MESH)
+
+    pending, shared = [], []
     def send(part, stage, kind, gathered, where, halves, target):
-        ref = window(part, gathered, where, halves)
-        copy = pltpu.make_async_remote_copy(
-            src_ref=ref, dst_ref=ref, send_sem=send_sem.at[part, stage, kind], recv_sem=recv_sem.at[part, stage, kind],
-            device_id=device(target), device_id_type=MESH)
-        copy.start()
-        pending.append(copy)
+        src = own_ref.at[pl.ds(part * rows + halves * half, half)] if stage == 0 and kind < 4 else None
+        one = copy(part, stage, kind, gathered, where, halves, target, send_sem, recv_sem, src)
+        one.start()
+        pending.append(one)
     def arrive(part, stage, kind, gathered, where, halves):
-        ref = window(part, gathered, where, halves)
-        pltpu.make_async_remote_copy(
-            src_ref=ref, dst_ref=ref, send_sem=send_sem.at[part, stage, kind], recv_sem=recv_sem.at[part, stage, kind],
-            device_id=device(at), device_id_type=MESH).wait_recv()
-    shared = []
+        copy(part, stage, kind, gathered, where, halves, twin(at), send_sem, recv_sem).wait_recv()
     def share(part, stage, kind, gathered, where, halves):
-        ref = window(part, gathered, where, halves)
-        copy = pltpu.make_async_remote_copy(
-            src_ref=ref, dst_ref=ref, send_sem=twin_send.at[part, stage, kind], recv_sem=twin_recv.at[part, stage, kind],
-            device_id=device(twin(at)), device_id_type=MESH)
-        copy.start()
-        shared.append((copy, part, stage, kind, gathered, where, halves))
-
-    mine = all_ref.at[at["z"], at["y"], at["x"], at["c"]]
-    copy = pltpu.make_async_copy(own_ref, mine, local_sem)
-    copy.start()
-    copy.wait()
-    for part in range(3):
+        one = copy(part, stage, kind, gathered, where, halves, twin(at), twin_send, twin_recv)
+        one.start()
+        shared.append((one, part, stage, kind, gathered, where, halves))
+
+    def around(part, stage):
+        names = ORDERS[part // SLICES]
+        axis, gathered = names[stage], names[:stage]
+        return gathered, moved(at, axis, 1), moved(at, axis, SIDE - 1), moved(at, axis, 2)
+    def begin(part, stage):
+        gathered, up, down, _ = around(part, stage)
+        send(part, stage, 0, gathered, at, 0, up)
+        send(part, stage, 1, gathered, at, 1, down)
+        send(part, stage, 2, gathered, at, 1, up)
+        send(part, stage, 3, gathered, at, 0, down)
+    def relay(part, stage):
+        gathered, up, down, _ = around(part, stage)
+        arrive(part, stage, 0, gathered, down, 0)
+        send(part, stage, 4, gathered, down, 0, up)
+        share(part, stage, 0, gathered, down, 0)
+        arrive(part, stage, 1, gathered, up, 1)
+        send(part, stage, 5, gathered, up, 1, down)
+        share(part, stage, 1, gathered, up, 1)
+    def finish(part, stage, kinds):
+        gathered, up, down, far = around(part, stage)
+        for kind in kinds:
+            where, halves = ((down, 1), (up, 0), (far, 0), (far, 1))[kind - 2]
+            arrive(part, stage, kind, gathered, where, halves)
+            share(part, stage, kind, gathered, where, halves)
+
+    parts = [[axis * SLICES + piece for axis in range(3)] for piece in range(SLICES)]
+    local = pltpu.make_async_copy(own_ref, all_ref.at[at["z"], at["y"], at["x"], at["c"]], local_sem)
+    local.start()
+    for group in parts:
+        for part in group:
+            begin(part, 0)
+    local.wait()
+    for part in range(3 * SLICES):
         share(part, 3, 0, (), at, None)
     for stage in range(3):
-        for part in range(3):
-            axis, gathered = ORDERS[part][stage], ORDERS[part][:stage]
-            up, down = moved(at, axis, 1), moved(at, axis, SIDE - 1)
-            send(part, stage, 0, gathered, at, 0, up)
-            send(part, stage, 1, gathered, at, 1, down)
-            send(part, stage, 2, gathered, at, 1, up)
-            send(part, stage, 3, gathered, at, 0, down)
-        for part in range(3):
-            axis, gathered = ORDERS[part][stage], ORDERS[part][:stage]
-            up, down = moved(at, axis, 1), moved(at, axis, SIDE - 1)
-            arrive(part, stage, 0, gathered, down, 0)
-            send(part, stage, 4, gathered, down, 0, up)
-            share(part, stage, 0, gathered, down, 0)
-            arrive(part, stage, 1, gathered, up, 1)
-            send(part, stage, 5, gathered, up, 1, down)
-            share(part, stage, 1, gathered, up, 1)
-        for part in range(3):
-            axis, gathered = ORDERS[part][stage], ORDERS[part][:stage]
-            up, down, far = moved(at, axis, 1), moved(at, axis, SIDE - 1), moved(at, axis, 2)
-            for kind, where, halves in ((2, down, 1), (3, up, 0), (4, far, 0), (5, far, 1)):
-                arrive(part, stage, kind, gathered, where, halves)
-                share(part, stage, kind, gathered, where, halves)
-    for copy in pending:
-        copy.wait_send()
-    for copy, part, stage, kind, gathered, where, halves in shared:
-        copy.wait_send()
-        ref = window(part, gathered, twin(where), halves)
-        pltpu.make_async_remote_copy(
-            src_ref=ref, dst_ref=ref, send_sem=twin_send.at[part, stage, kind], recv_sem=twin_recv.at[part, stage, kind],
-            device_id=device(twin(at)), device_id_type=MESH).wait_recv()
+        for group in parts:
+            for part in group:
+                relay(part, stage)
+            for part in group:
+                finish(part, stage, (2, 3))
+            for part in group:
+                finish(part, stage, (4, 5))
+                if stage < 2:
+                    begin(part, stage + 1)
+    for one in pending:
+        one.wait_send()
+    for one, part, stage, kind, gathered, where, halves in shared:
+        one.wait_send()
+        copy(part, stage, kind, gathered, twin(where), halves, twin(at), twin_send, twin_recv).wait_recv()
 
 
 def adapt_kernel(count_ref, snap_ref, chosen_ref, steer_ref, all_ref, packed, weights, diag, cov, rhs, inv, go, *scratch):
@@ -464,7 +493,7 @@
             pltpu.VMEM((SIDE, SIDE, SIDE, 8, T), f32), pltpu.VMEM((3, SIDE, SIDE, SIDE, PACKED, T), f32), *boxes,
             sem((SIDE,)), sem((SIDE,)), sem((SIDE,)), sem((3, 3)), sem((3, 3)),
             sem((3, 6, SIDE)), sem((3, 6, SIDE)), sem((3, 2, 6)), sem((3, 2, 6)),
-            sem, sem((3, 3, 6)), sem((3, 3, 6)), sem((3, 4, 6)), sem((3, 4, 6)),
+            sem, *[sem((3 * SLICES, n, 6)) for n in (3, 3, 4, 4)],
         ],
         compiler_params=pltpu.CompilerParams(collective_id=1, has_side_effects=True, vmem_limit_bytes=67000000),
         name="adapt",
@@ -476,7 +505,7 @@
     for b in range(snap_ref.shape[0]):
         out_ref[b] = jnp.dot(snap_ref[b], weight_ref[b], preferred_element_type=jnp.float32).astype(out_ref.dtype)
 
-def beams(snapshots, weights, step=16):
+def beams(snapshots, weights, step=32):
     bins, gates, channels = snapshots.shape
     looks = weights.shape[2]
     return pl.pallas_call(
@@ -491,7 +520,7 @@
 
 def body(snapshots, steering, train_list, train_count):
     chosen = selection(train_list, train_count).astype(jnp.float32)
-    weights = adapt(snapshots, jnp.broadcast_to(chosen, (8, BLOCK)), train_count, steering[0])
+    weights = adapt(snapshots, chosen, train_count, steering[0])
     return beams(snapshots, weights)
 
 

time: 216 us -> 187 us (0.87)
  Pallas kernels: 214 us -> 185 us
    pallas_call x1, Pallas kernels: 196 us -> 168 us  [adapt(): pl.pallas_call(adapt_kernel, out_shape=jax.ShapeDtypeStruct((SIDE, SIDE,...]
where the time goes in v5:
time: 187 us
  Pallas kernels  185 us (99%)
    pallas_call x1, Pallas kernels, adapt(): pl.pallas_call(adapt_kernel, out_shape=jax.ShapeDtypeStruct((SIDE, SIDE,...  168 us
    pallas_call x1, Pallas kernels, beams(): pl.pallas_call(apply_kernel, grid=(bins // step,), out_shape=jax.ShapeDty...  16.7 us

profile of v5, /device:TPU:1, one launch (start us, length us, event | category | flops | bytes accessed | tf_op | source)
XLA Modules:
  0.0 186.9 jit_solution(1418416067587467319)
XLA Ops:
  0.7 0.8 convert_reduce_fusion
  1.4 0.5 convert_bitcast_fusion.chosen_ref
  2.0 168.3 %adapt.1 = bf16[4,4,4,2,384,256]{5,4,3,2,1,0:T(8,128)(2,1)} custom-call(s32[1]{0:T(128)} %copy.5.count_ref, bf16[4,4,4,2,128,384]{5,4,3,2,1,0:T(8,128)(2,1)} %bitcast.9, f32[1,128]{1,0:T(1,128)} %convert_bitcast_fusion.chosen_ref, bf16[384,256]{1,0:T(8,128)(2,1)} %bitcast.10), custom_call_target="tpu_custom_call" | custom-call | tf_op jit(solution)/shard_map/adapt/pallas_call | solution.py:483
  170.2 16.7 %beams.1 = bf16[128,128,256]{2,1,0:T(8,128)(2,1)} custom-call(bf16[128,128,384]{2,1,0:T(8,128)(2,1)} %snap_ref.1, bf16[128,384,256]{2,1,0:T(8,128)(2,1)} %bitcast.8), custom_call_target="tpu_custom_call" | custom-call | tf_op jit(solution)/shard_map/beams/pallas_call | solution.py:511
  (1 shorter events, 0.0 us)

commit v6 on v5

--- a/solution.py
+++ b/solution.py
@@ -403,7 +403,7 @@
 
     pending, shared = [], []
     def send(part, stage, kind, gathered, where, halves, target):
-        src = own_ref.at[pl.ds(part * rows + halves * half, half)] if stage == 0 and kind < 4 else None
+        src = own_ref.at[pl.ds(part * rows + halves * half, half)] if stage == 0 else None
         one = copy(part, stage, kind, gathered, where, halves, target, send_sem, recv_sem, src)
         one.start()
         pending.append(one)
@@ -419,18 +419,23 @@
         axis, gathered = names[stage], names[:stage]
         return gathered, moved(at, axis, 1), moved(at, axis, SIDE - 1), moved(at, axis, 2)
     def begin(part, stage):
-        gathered, up, down, _ = around(part, stage)
+        gathered, up, down, far = around(part, stage)
         send(part, stage, 0, gathered, at, 0, up)
         send(part, stage, 1, gathered, at, 1, down)
         send(part, stage, 2, gathered, at, 1, up)
         send(part, stage, 3, gathered, at, 0, down)
+        if stage == 0:
+            send(part, stage, 4, gathered, at, 0, far)
+            send(part, stage, 5, gathered, at, 1, far)
     def relay(part, stage):
         gathered, up, down, _ = around(part, stage)
         arrive(part, stage, 0, gathered, down, 0)
-        send(part, stage, 4, gathered, down, 0, up)
+        if stage:
+            send(part, stage, 4, gathered, down, 0, up)
         share(part, stage, 0, gathered, down, 0)
         arrive(part, stage, 1, gathered, up, 1)
-        send(part, stage, 5, gathered, up, 1, down)
+        if stage:
+            send(part, stage, 5, gathered, up, 1, down)
         share(part, stage, 1, gathered, up, 1)
     def finish(part, stage, kinds):
         gathered, up, down, far = around(part, stage)
@@ -501,19 +506,53 @@
     return whole.reshape(bins, channels, looks)
 
 
-def apply_kernel(snap_ref, weight_ref, out_ref):
-    for b in range(snap_ref.shape[0]):
-        out_ref[b] = jnp.dot(snap_ref[b], weight_ref[b], preferred_element_type=jnp.float32).astype(out_ref.dtype)
-
-def beams(snapshots, weights, step=32):
+def apply_kernel(snap_hbm, weight_hbm, out_hbm, snaps, weights, outs, snap_sem, weight_sem, out_sem):
+    chunks = snap_sem.shape[0]
+    step = snaps.shape[0] // chunks
+
+    def part(n):
+        return pl.ds(pl.multiple_of(n * step, step), step)
+    def snap_copy(n):
+        return pltpu.make_async_copy(snap_hbm.at[part(n)], snaps.at[part(n)], snap_sem.at[n])
+    def weight_copy(n):
+        return pltpu.make_async_copy(weight_hbm.at[part(n)], weights.at[part(n)], weight_sem.at[n])
+    def out_copy(n):
+        return pltpu.make_async_copy(outs.at[part(n)], out_hbm.at[part(n)], out_sem.at[n])
+
+    def fetch(n, carry):
+        snap_copy(n).start()
+        weight_copy(n).start()
+        return carry
+    lax.fori_loop(0, chunks, fetch, 0)
+    def multiply(n, carry):
+        snap_copy(n).wait()
+        weight_copy(n).wait()
+        for b in range(step):
+            at = n * step + b
+            outs[at] = jnp.dot(snaps[at], weights[at], preferred_element_type=jnp.float32).astype(outs.dtype)
+        out_copy(n).start()
+        return carry
+    lax.fori_loop(0, chunks, multiply, 0)
+    def drain(n, carry):
+        out_copy(n).wait()
+        return carry
+    lax.fori_loop(0, chunks, drain, 0)
+
+
+def beams(snapshots, weights, chunks=16):
     bins, gates, channels = snapshots.shape
     looks = weights.shape[2]
+    bf16, sem, whole = jnp.bfloat16, pltpu.SemaphoreType.DMA, pl.BlockSpec(memory_space=pl.ANY)
     return pl.pallas_call(
         apply_kernel,
-        grid=(bins // step,),
-        out_shape=jax.ShapeDtypeStruct((bins, gates, looks), jnp.bfloat16),
-        in_specs=[pl.BlockSpec((step, gates, channels), lambda i: (i, 0, 0)), pl.BlockSpec((step, channels, looks), lambda i: (i, 0, 0))],
-        out_specs=pl.BlockSpec((step, gates, looks), lambda i: (i, 0, 0)),
+        out_shape=jax.ShapeDtypeStruct((bins, gates, looks), bf16),
+        in_specs=[whole, whole],
+        out_specs=whole,
+        scratch_shapes=[
+            pltpu.VMEM((bins, gates, channels), bf16), pltpu.VMEM((bins, channels, looks), bf16), pltpu.VMEM((bins, gates, looks), bf16),
+            sem((chunks,)), sem((chunks,)), sem((chunks,)),
+        ],
+        compiler_params=pltpu.CompilerParams(vmem_limit_bytes=60 * 1024 * 1024),
         name="beams",
     )(snapshots, weights)
 

time: 187 us -> 185 us (0.989)
  Pallas kernels: 185 us -> 183 us
where the time goes in v6:
time: 185 us
  Pallas kernels  183 us (99%)
    pallas_call x1, Pallas kernels, adapt(): pl.pallas_call(adapt_kernel, out_shape=jax.ShapeDtypeStruct((SIDE, SIDE,...  166 us
    pallas_call x1, Pallas kernels, beams(): pl.pallas_call(apply_kernel, out_shape=jax.ShapeDtypeStruct((bins, gates,...  16.1 us

profile of v6, /device:TPU:1, one launch (start us, length us, event | category | flops | bytes accessed | tf_op | source)
XLA Modules:
  0.0 184.7 jit_solution(994053130331475501)
XLA Ops:
  0.7 0.8 convert_reduce_fusion
  1.4 0.5 convert_bitcast_fusion.chosen_ref
  2.0 166.4 %adapt.1 = bf16[4,4,4,2,384,256]{5,4,3,2,1,0:T(8,128)(2,1)} custom-call(s32[1]{0:T(128)} %copy.5.count_ref, bf16[4,4,4,2,128,384]{5,4,3,2,1,0:T(8,128)(2,1)} %bitcast.9, f32[1,128]{1,0:T(1,128)} %convert_bitcast_fusion.chosen_ref, bf16[384,256]{1,0:T(8,128)(2,1)} %bitcast.10), custom_call_target="tpu_custom_call" | custom-call | tf_op jit(solution)/shard_map/adapt/pallas_call | solution.py:488
  168.4 16.1 %beams.1 = bf16[128,128,256]{2,1,0:T(8,128)(2,1)} custom-call(bf16[128,128,384]{2,1,0:T(8,128)(2,1)} %snap_hbm.1, bf16[128,384,256]{2,1,0:T(8,128)(2,1)} %bitcast.8), custom_call_target="tpu_custom_call" | custom-call | tf_op jit(solution)/shard_map/beams/pallas_call | solution.py:546
  (1 shorter events, 0.0 us)

commit v7 on v6

--- a/solution.py
+++ b/solution.py
@@ -9,12 +9,12 @@
 LOADING = 0.1
 
 
-def selection(train_list, train_count):
-    block_total = train_list.shape[1]
-    position = lax.broadcasted_iota(jnp.int32, (1, block_total, 1), 1)
-    block_ids = lax.broadcasted_iota(jnp.int32, (1, 1, block_total), 2)
-    matches = (train_list[:, :, None] == block_ids) & (position < train_count[:, None, None])
-    return jnp.sum(matches.astype(jnp.int32), axis=1)
+def selection(order, count):
+    block = lax.broadcasted_iota(jnp.int32, (BLOCK, BLOCK), 0)
+    position = lax.broadcasted_iota(jnp.int32, (BLOCK, BLOCK), 1)
+    matches = jnp.where((order == block) & (position < count), 1.0, 0.0)
+    ones = jnp.ones((8, BLOCK), jnp.float32)
+    return lax.dot_general(ones, matches, (((1,), (1,)), ((), ())), preferred_element_type=jnp.float32)
 
 
 HI = lax.Precision.HIGHEST
@@ -142,7 +142,7 @@
     t22 = jnp.where((i == j) & (i < HALF), ridge, jnp.where(keep, mixed, mixed.T))
     return t00, packed[0, :T], t11, packed[2, :T], packed[1, :T].T, t22
 
-def reduce_phase(at, snap_ref, chosen_ref, out_ref, go, own, other, marks, grams, far1, down1, up1, far2, down2, up2, far3, down3, up3,
+def reduce_phase(at, count_ref, snap_ref, order_ref, out_ref, go, own, other, marks, grams, far1, down1, up1, far2, down2, up2, far3, down3, up3,
                   own_sem, twin_send, twin_recv, mark_send, mark_recv, send1, recv1, send2, recv2):
     twin_at = twin(at)
     me = ((at["z"] * SIDE + at["y"]) * SIDE + at["x"]) * 2
@@ -170,7 +170,7 @@
     for z in order:
         twin_copy(z).start()
         own_copy(z).start()
-    marks[at["z"], at["y"], at["x"]] = jnp.broadcast_to(chosen_ref[...], (8, T))
+    marks[at["z"], at["y"], at["x"]] = selection(order_ref[...], count_ref[0])
     for stage in range(3):
         for kind in range(3):
             mark_copy(stage, kind).start()
@@ -470,15 +470,15 @@
         copy(part, stage, kind, gathered, twin(where), halves, twin(at), twin_send, twin_recv).wait_recv()
 
 
-def adapt_kernel(count_ref, snap_ref, chosen_ref, steer_ref, all_ref, packed, weights, diag, cov, rhs, inv, go, *scratch):
+def adapt_kernel(count_ref, snap_ref, order_ref, steer_ref, all_ref, packed, weights, diag, cov, rhs, inv, go, *scratch):
     at = place()
     greet(at)
-    reduce_phase(at, snap_ref, chosen_ref, packed, go, *scratch[:-5])
+    reduce_phase(at, count_ref, snap_ref, order_ref, packed, go, *scratch[:-5])
     solve_phase(count_ref, packed, steer_ref, weights, diag, cov, rhs, inv)
     gather_phase(at, weights, all_ref, *scratch[-5:])
 
 
-def adapt(snapshots, chosen, train_count, steering):
+def adapt(snapshots, train_list, train_count, steering):
     bins, gates, channels = snapshots.shape
     looks = steering.shape[1]
     split = snapshots.reshape(SIDE, SIDE, SIDE, 2, gates, channels)
@@ -502,7 +502,7 @@
         ],
         compiler_params=pltpu.CompilerParams(collective_id=1, has_side_effects=True, vmem_limit_bytes=67000000),
         name="adapt",
-    )(train_count, split, chosen, steering)
+    )(train_count, split, train_list, steering)
     return whole.reshape(bins, channels, looks)
 
 
@@ -558,8 +558,7 @@
 
 
 def body(snapshots, steering, train_list, train_count):
-    chosen = selection(train_list, train_count).astype(jnp.float32)
-    weights = adapt(snapshots, chosen, train_count, steering[0])
+    weights = adapt(snapshots, train_list, train_count, steering[0])
     return beams(snapshots, weights)
 
 

time: 185 us -> 184 us (level)
  no operation moved by 1% of the time
where the time goes in v7:
time: 184 us
  Pallas kernels  183 us (99%)
    pallas_call x1, Pallas kernels, adapt(): pl.pallas_call(adapt_kernel, out_shape=jax.ShapeDtypeStruct((SIDE, SIDE,...  167 us
    pallas_call x1, Pallas kernels, beams(): pl.pallas_call(apply_kernel, out_shape=jax.ShapeDtypeStruct((bins, gates,...  16.1 us

profile of v7, /device:TPU:1, one launch (start us, length us, event | category | flops | bytes accessed | tf_op | source)
XLA Modules:
  0.0 183.6 jit_solution(14932726160893478753)
XLA Ops:
  0.7 166.6 %adapt.1 = bf16[4,4,4,2,384,256]{5,4,3,2,1,0:T(8,128)(2,1)} custom-call(s32[1]{0:T(128)S(6)} %copy.5.count_ref, bf16[4,4,4,2,128,384]{5,4,3,2,1,0:T(8,128)(2,1)} %bitcast.4, s32[1,128]{1,0:T(1,128)} %order_ref.1, bf16[384,256]{1,0:T(8,128)(2,1)} %bitcast.5), custom_call_target="tpu_custom_call" | custom-call | tf_op jit(solution)/shard_map/adapt/pallas_call | solution.py:488
  167.3 16.1 %beams.1 = bf16[128,128,256]{2,1,0:T(8,128)(2,1)} custom-call(bf16[128,128,384]{2,1,0:T(8,128)(2,1)} %snap_hbm.1, bf16[128,384,256]{2,1,0:T(8,128)(2,1)} %bitcast.3), custom_call_target="tpu_custom_call" | custom-call | tf_op jit(solution)/shard_map/beams/pallas_call | solution.py:546
